TPU v7x, 512 devices: a whole 4x4x16 slice. The times are simulated.
512 devices in a mesh: gx: 64 (over z, y), gy: 8 (over x, core).
Axes of the slice: x: 4, y: 4, z: 16, core: 2. Of those that a mesh axis runs over, the one named last changes fastest.
Arguments:
- volume: bfloat16 [128, 64, 4096], P('gx', 'gy'), may hold values from -130 to 130
- conv_first: bfloat16 [1728, 64], replicated, may hold values from -0.96225045 to 0.96225045
- gain: float32 [64], replicated, may hold values from 0.5 to 1.5
- shift: float32 [64], replicated, may hold values from -3 to 3
- conv_second: bfloat16 [1728, 64], replicated, may hold values from -0.15625 to 0.15625
- bias_second: float32 [64], replicated, may hold values from -3 to 3
Outputs:
- result: bfloat16 [128, 64, 4096], P('gx', 'gy')
All inputs are finite; a program needn't handle non-finite values.
Results may differ from a plain program's by a relative error of at most 0.004.
Values may be sent and summed in bfloat16 or wider, within the bound.
No kernel may reach another device: no remote copies, remote signals or barrier semaphores. Data moves between devices by JAX's collectives and lax.ppermute only.
A program may use at most 64 MiB of HBM per device.

v0:
```python
import functools

import jax
import jax.numpy as jnp
from jax import lax
from jax.sharding import Mesh
from jax.sharding import PartitionSpec as P

NEWTON = 5
GX_GY = ("gx_0", "gx_1", "gy_0", "gy_1")
GX = ("gx_0", "gx_1")
GY = ("gy_0", "gy_1")


def by_axis(value, axes):
    return functools.reduce(lax.psum, axes, value)


def padded_2(block, sides, width):
    for axis, dim in sides:
        count = lax.axis_size(axis)
        forward = [(i, i + 1) for i in range(count - 1)]
        backward = [(target, source) for source, target in forward]
        low = lax.ppermute(
            lax.slice_in_dim(block, block.shape[dim] - width, None, axis=dim), axis, forward
        )
        high = lax.ppermute(lax.slice_in_dim(block, 0, width, axis=dim), axis, backward)
        block = jnp.concatenate([low, block, high], axis=dim)
    return block


def convolve(padded, weights, depth):
    width = weights.shape[1]
    rows_x = padded.shape[0] - 2
    rows_y = padded.shape[1] - 2
    vol = padded.reshape(rows_x + 2, rows_y + 2, depth, width)
    zpad = jnp.pad(vol, ((0, 0), (0, 0), (1, 1), (0, 0)))
    zcat = jnp.concatenate(
        [zpad[:, :, 0:depth], zpad[:, :, 1 : depth + 1], zpad[:, :, 2 : depth + 2]], axis=3
    )
    acc = jnp.zeros((rows_x * rows_y * depth, width), jnp.float32)
    for dx in range(3):
        for dy in range(3):
            tap = zcat[dx : dx + rows_x, dy : dy + rows_y].reshape(-1, 3 * width)
            first = (dx * 3 + dy) * 3 * width
            acc = acc + jnp.dot(
                tap, weights[first : first + 3 * width], preferred_element_type=jnp.float32
            )
    return acc


def newton_whiten(sigma):
    dims = sigma.shape[0]
    trace_value = jnp.trace(sigma)
    normed = sigma / trace_value
    proj = jnp.eye(dims, dtype=jnp.float32)
    for step in range(NEWTON):
        cube = jnp.dot(
            jnp.dot(proj, proj, precision=lax.Precision.HIGHEST),
            proj,
            precision=lax.Precision.HIGHEST,
        )
        proj = 1.5 * proj - 0.5 * jnp.dot(cube, normed, precision=lax.Precision.HIGHEST)
    return proj / jnp.sqrt(trace_value)


def statistics(hidden, count):
    width = hidden.shape[1]
    ident = jnp.eye(width, dtype=jnp.float32)
    local_sum = jnp.sum(hidden, axis=0)
    local_gram = jnp.dot(hidden.T, hidden, precision=lax.Precision.HIGHEST)
    total_sum, total_gram = (by_axis(local_sum, GX_GY), by_axis(local_gram, GX_GY))
    mean = total_sum / count
    sigma = total_gram / count - mean[:, None] * mean[None, :] + 1e-05 * ident
    return (mean, newton_whiten(sigma))


def activate(hidden, mean, whiten, gain, shift):
    normalized = jnp.dot(hidden - mean[None, :], whiten, precision=lax.Precision.HIGHEST)
    return jnp.maximum(gain[None, :] * normalized + shift[None, :], 0.0)


def inside_grid(rows_x, rows_y):
    pos_x = lax.axis_index(GX) * rows_x + jnp.arange(rows_x + 2, dtype=jnp.int32) - 1
    pos_y = lax.axis_index(GY) * rows_y + jnp.arange(rows_y + 2, dtype=jnp.int32) - 1
    inside_x = ((pos_x >= 0) & (pos_x < rows_x * lax.axis_size(GX))).astype(jnp.float32)
    inside_y = ((pos_y >= 0) & (pos_y < rows_y * lax.axis_size(GY))).astype(jnp.float32)
    return (inside_x[:, None] * inside_y[None, :]).reshape(rows_x + 2, rows_y + 2, 1, 1)


def rimmed_act(rimmed_rows, mean, whiten, gain, shift, rows_x, rows_y, depth):
    width = mean.shape[0]
    act = activate(rimmed_rows, mean, whiten, gain, shift)
    act = act.reshape(rows_x + 2, rows_y + 2, depth, width) * inside_grid(rows_x, rows_y)
    return act.astype(jnp.bfloat16).reshape(rows_x + 2, rows_y + 2, depth * width)


def local(volume, conv_first, gain, shift, conv_second, bias_second):
    width = bias_second.shape[0]
    rows_x, rows_y, merged = volume.shape
    depth = merged // width
    count = float(rows_x * lax.axis_size(GX) * rows_y * lax.axis_size(GY) * depth)
    rim_depth = 2
    padded = padded_2(volume, ((GX, 0), (GY, 1)), rim_depth)
    hidden_all = convolve(padded, conv_first, depth)
    widened = hidden_all.reshape(rows_x + 2, rows_y + 2, depth, width)
    hidden = widened[1:-1, 1:-1].reshape(-1, width)
    mean, whiten = statistics(hidden, count)
    act_padded = rimmed_act(hidden_all, mean, whiten, gain, shift, rows_x, rows_y, depth)
    out = convolve(act_padded, conv_second, depth) + bias_second[None, :]
    return out.astype(jnp.bfloat16).reshape(rows_x, rows_y, merged)


def solution(mesh):
    torus = Mesh(mesh.devices.reshape(16, 4, 4, 2), ("gx_0", "gx_1", "gy_0", "gy_1"))
    placed = (P(GX, GY, None), P(), P(), P(), P(), P())
    return jax.shard_map(
        local, mesh=torus, in_specs=placed, out_specs=P(GX, GY, None), check_vma=False
    )
```

profile of v0, /device:TPU:1, one launch (start us, length us, event | category | flops | bytes accessed | tf_op | source)
XLA Modules:
  0.0 148.5 jit_solution(18224045949213381677)
XLA Ops:
  0.0 4.0 %collective-permute-start = (bf16[2,8,4096]{2,1,0:T(8,128)(2,1)}, bf16[2,8,4096]{2,1,0:T(8,128)(2,1)S(1)}, u32[]{:S(2)}, u32[]{:S(2)}) collective-permute-start(bf16[2,8,4096]{2,1,0:T(8,128)(2,1)} %param.6), channel_id=1, source_target_pairs={{0,8},{8,16},{16,24},{24,32},{32,40},{40,48},{48,56},{56,64},{64,7... | collective-permute-start | bytes 393224 | tf_op jit(solution)/shard_map/ppermute | solution.py:24
  4.0 1.3 collective-permute-start.1
  5.7 0.6 collective-permute-done
  6.3 0.9 constant_dynamic-update-slice_fusion.1
  7.2 2.8 %collective-permute-done.1 = bf16[2,8,4096]{2,1,0:T(8,128)(2,1)S(1)} collective-permute-done((bf16[2,8,4096]{2,1,0:T(8,128)(2,1)}, bf16[2,8,4096]{2,1,0:T(8,128)(2,1)S(1)}, u32[]{:S(2)}, u32[]{:S(2)}) %collective-permute-start.1) | collective-permute-done | bytes 131104 | tf_op jit(solution)/shard_map/ppermute | solution.py:27
  10.1 5.1 %collective-permute-start.2 = (bf16[6,2,4096]{2,1,0:T(2,128)(2,1)S(1)}, bf16[6,2,4096]{2,1,0:T(2,128)(2,1)S(1)}, u32[]{:S(2)}, u32[]{:S(2)}) collective-permute-start(bf16[6,2,4096]{2,1,0:T(2,128)(2,1)S(1)} %get-tuple-element.35), channel_id=1, source_target_pairs={{0,1},{1,2},{2,3},{3,4},{4,5},{5,6},{6,7},{8,9},{9,10},{10,11},{11... | collective-permute-start | bytes 294920 | tf_op jit(solution)/shard_map/ppermute | solution.py:24
  15.2 3.4 %collective-permute-start.3 = (bf16[6,2,4096]{2,1,0:T(2,128)(2,1)S(1)}, bf16[6,2,4096]{2,1,0:T(2,128)(2,1)S(1)}, u32[]{:S(2)}, u32[]{:S(2)}) collective-permute-start(bf16[6,2,4096]{2,1,0:T(2,128)(2,1)S(1)} %get-tuple-element.36), channel_id=1, source_target_pairs={{1,0},{2,1},{3,2},{4,3},{5,4},{6,5},{7,6},{9,8},{10,9},{11,10},{12... | collective-permute-start | bytes 294920 | tf_op jit(solution)/shard_map/ppermute | solution.py:27
  18.7 2.5 %collective-permute-done.3 = bf16[6,2,4096]{2,1,0:T(2,128)(2,1)S(1)} collective-permute-done((bf16[6,2,4096]{2,1,0:T(2,128)(2,1)S(1)}, bf16[6,2,4096]{2,1,0:T(2,128)(2,1)S(1)}, u32[]{:S(2)}, u32[]{:S(2)}) %collective-permute-start.3) | collective-permute-done | bytes 98336 | tf_op jit(solution)/shard_map/ppermute | solution.py:27
  21.5 1.2 reshape.118
  22.8 1.0 pad_slice_fusion.1
  23.8 1.1 pad_maximum_fusion
  25.0 2.1 %fusion.41 = (bf16[4,10,64,192]{3,2,1,0:T(8,128)(2,1)S(1)}, bf16[4,10,64,192]{3,2,1,0:T(8,128)(2,1)S(1)}, bf16[4,10,64,192]{3,2,1,0:T(8,128)(2,1)S(1)}, bf16[4,1...) fusion(bf16[6,12,64,192]{3,2,1,0:T(8,128)(2,1)S(1)} %pad_maximu, ...), kind=kLoop, calls=%fused_computation.78 | loop fusion | bytes 17694720 | tf_op jit(solution)/shard_map/slice | solution.py:44
  27.6 0.5 convolution_add_fusion.7
  28.7 0.5 convolution_add_fusion.5
  29.7 0.5 convolution_add_fusion.3
  30.8 0.5 convolution_add_fusion.1
  32.2 1.0 convolution_bitcast_fusion
  33.5 48.3 %all-reduce.2 = (f32[64,64]{1,0:T(8,128)S(1)}, f32[64]{0:T(128)S(1)}) all-reduce(f32[64,64]{1,0:T(8,128)S(1)} %convolution_bitcast_fusion, f32[64]{0:T(128)S(1)} %slice_reduce_fusion), channel_id=1, replica_groups=mesh['gx_0'=16,'gx_1'=4,'gy_0'=4,'gy_1'=2] {'gx_0'}, use_global_device_ids=true, to_apply=%region_5.6 | all-reduce | flops 4160 | bytes 33280 | tf_op jit(solution)/shard_map/psum | solution.py:16
  81.8 14.9 %all-reduce.4 = (f32[64,64]{1,0:T(8,128)S(1)}, f32[64]{0:T(128)S(1)}) all-reduce(f32[64,64]{1,0:T(8,128)S(1)} %get-tuple-element.5, f32[64]{0:T(128)S(1)} %get-tuple-element.6), channel_id=1, replica_groups=mesh['gx_0'=16,'gx_1'=4,'gy_0'=4,'gy_1'=2] {'gx_1'}, use_global_device_ids=true, to_apply=%region_6.7 | all-reduce | flops 4160 | bytes 33280 | tf_op jit(solution)/shard_map/psum | solution.py:16
  96.7 13.0 %all-reduce.3 = (f32[64,64]{1,0:T(8,128)S(1)}, f32[64]{0:T(128)S(1)}) all-reduce(f32[64,64]{1,0:T(8,128)S(1)} %get-tuple-element.9, f32[64]{0:T(128)S(1)} %get-tuple-element.10), channel_id=1, replica_groups=mesh['gx_0'=16,'gx_1'=4,'gy_0'=4,'gy_1'=2] {'gy_0'}, use_global_device_ids=true, to_apply=%region_7.8 | all-reduce | flops 4160 | bytes 33280 | tf_op jit(solution)/shard_map/psum | solution.py:16
  109.7 24.3 %all-reduce.5 = (f32[64,64]{1,0:T(8,128)S(1)}, f32[64]{0:T(128)S(1)}) all-reduce(f32[64,64]{1,0:T(8,128)S(1)} %get-tuple-element.7, f32[64]{0:T(128)S(1)} %get-tuple-element.8), channel_id=1, replica_groups=mesh['gx_0'=16,'gx_1'=4,'gy_0'=4,'gy_1'=2] {'gy_1'}, use_global_device_ids=true, to_apply=%region_8.9 | all-reduce | flops 4160 | bytes 33280 | tf_op jit(solution)/shard_map/psum | solution.py:16
  134.0 0.7 select_reduce_fusion
  135.4 0.9 fusion.9
  136.6 0.9 fusion.8
  137.8 0.9 fusion.7
  139.1 0.9 fusion.6
  140.3 0.9 fusion.5
  141.2 0.8 fusion.1
  142.6 0.5 pad_slice_fusion.3
  143.2 0.7 pad_maximum_fusion.1
  143.8 0.6 fusion.42
  147.6 0.9 reshape.139
  (48 shorter events, 9.0 us)
Async XLA Ops:
  0.0 6.3 %collective-permute-start = (bf16[2,8,4096]{2,1,0:T(8,128)(2,1)}, bf16[2,8,4096]{2,1,0:T(8,128)(2,1)S(1)}, u32[]{:S(2)}, u32[]{:S(2)}) collective-permute-start(bf16[2,8,4096]{2,1,0:T(8,128)(2,1)} %param.6), channel_id=1, source_target_pairs={{0,8},{8,16},{16,24},{24,32},{32,40},{40,48},{48,56},{56,64},{64,7... | collective-permute-start | bytes 393224 | tf_op jit(solution)/shard_map/ppermute | solution.py:24
  4.0 5.9 %collective-permute-start.1 = (bf16[2,8,4096]{2,1,0:T(8,128)(2,1)}, bf16[2,8,4096]{2,1,0:T(8,128)(2,1)S(1)}, u32[]{:S(2)}, u32[]{:S(2)}) collective-permute-start(bf16[2,8,4096]{2,1,0:T(8,128)(2,1)} %param.6), channel_id=1, source_target_pairs={{8,0},{16,8},{24,16},{32,24},{40,32},{48,40},{56,48},{64,56},{72,6... | collective-permute-start | bytes 393224 | tf_op jit(solution)/shard_map/ppermute | solution.py:27
  10.1 8.6 %collective-permute-start.2 = (bf16[6,2,4096]{2,1,0:T(2,128)(2,1)S(1)}, bf16[6,2,4096]{2,1,0:T(2,128)(2,1)S(1)}, u32[]{:S(2)}, u32[]{:S(2)}) collective-permute-start(bf16[6,2,4096]{2,1,0:T(2,128)(2,1)S(1)} %get-tuple-element.35), channel_id=1, source_target_pairs={{0,1},{1,2},{2,3},{3,4},{4,5},{5,6},{6,7},{8,9},{9,10},{10,11},{11... | collective-permute-start | bytes 294920 | tf_op jit(solution)/shard_map/ppermute | solution.py:24
  15.2 5.9 %collective-permute-start.3 = (bf16[6,2,4096]{2,1,0:T(2,128)(2,1)S(1)}, bf16[6,2,4096]{2,1,0:T(2,128)(2,1)S(1)}, u32[]{:S(2)}, u32[]{:S(2)}) collective-permute-start(bf16[6,2,4096]{2,1,0:T(2,128)(2,1)S(1)} %get-tuple-element.36), channel_id=1, source_target_pairs={{1,0},{2,1},{3,2},{4,3},{5,4},{6,5},{7,6},{9,8},{10,9},{11,10},{12... | collective-permute-start | bytes 294920 | tf_op jit(solution)/shard_map/ppermute | solution.py:27
  25.0 2.1 %copy-start.1 = (bf16[1728,64]{0,1:T(8,128)(2,1)S(1)}, bf16[1728,64]{0,1:T(8,128)(2,1)}, u32[]{:S(2)}) copy-start(bf16[1728,64]{0,1:T(8,128)(2,1)} %param.7) | copy-start | bytes 663556
  33.3 107.9 %copy-start.3 = (f32[64]{0:T(128)S(1)}, f32[64]{0:T(128)}, u32[]{:S(2)}) copy-start(f32[64]{0:T(128)} %param.9) | copy-start | bytes 772
  33.3 107.9 %copy-start.4 = (f32[64]{0:T(128)S(1)}, f32[64]{0:T(128)}, u32[]{:S(2)}) copy-start(f32[64]{0:T(128)} %param.8) | copy-start | bytes 772
  143.8 0.9 copy-start
  146.5 0.7 copy-start.2
where the time goes:
time: 149 us
  blocking collectives  101 us (68%)
  matrix products  15.1 us (10%)
  starting transfers between devices  13.8 us (9%)
  local copies, waits for them, and re-layouts  8.91 us (6%)
  waiting for transfers between devices  5.84 us (4%)
  other arithmetic  3.24 us (2%)
    psum x4, blocking collectives, by_axis(): return functools.reduce(lax.psum, axes, value)  101 us
    ppermute x2, starting transfers between devices, padded_2(): lax.ppermute(lax.slice_in_dim(block, block.shape[dim] - width, None, axis...  9.14 us
    dot_general x18, matrix products, convolve(): jnp.dot(tap, weights[first:first + 3 * width], preferred_element_type=jnp...  7.25 us
    ppermute x2, waiting for transfers between devices, padded_2(): lax.ppermute(lax.slice_in_dim(block, 0, width, axis=dim), axis, backward)  5.22 us
    ppermute x2, starting transfers between devices, padded_2(): lax.ppermute(lax.slice_in_dim(block, 0, width, axis=dim), axis, backward)  4.67 us
    dot_general x5, matrix products, newton_whiten(): jnp.dot(cube, normed, precision=lax.Precision.HIGHEST)  4.42 us
  transfers between devices with their start and end apart: 4, of which 3 were waited for; matrix products, arithmetic and copies ran while one was open for 1% of the time, Pallas kernels for 0%

commit v1 on v0

--- a/solution.py
+++ b/solution.py
@@ -7,13 +7,8 @@
 from jax.sharding import PartitionSpec as P
 
 NEWTON = 5
-GX_GY = ("gx_0", "gx_1", "gy_0", "gy_1")
 GX = ("gx_0", "gx_1")
 GY = ("gy_0", "gy_1")
-
-
-def by_axis(value, axes):
-    return functools.reduce(lax.psum, axes, value)
 
 
 def padded_2(block, sides, width):
@@ -64,12 +59,26 @@
     return proj / jnp.sqrt(trace_value)
 
 
+def exchange_sum(block, axes):
+    count = functools.reduce(lambda total, axis: total * lax.axis_size(axis), axes, 1)
+    copies = jnp.broadcast_to(block[None], (count,) + block.shape)
+    return jnp.sum(lax.all_to_all(copies, axes, 0, 0, tiled=True), axis=0)
+
+
+def total_over_mesh(local_sum, local_gram):
+    width = local_sum.shape[0]
+    row = jnp.concatenate([local_sum, jnp.zeros_like(local_sum)])
+    packed = jnp.concatenate([local_gram.reshape(-1, 1, 2 * width), row.reshape(1, 1, 2 * width)], axis=0)
+    total = exchange_sum(exchange_sum(packed, GX[:1]), GX[1:] + GY)
+    return total[-1, 0, :width], total[:-1].reshape(width, width)
+
+
 def statistics(hidden, count):
     width = hidden.shape[1]
     ident = jnp.eye(width, dtype=jnp.float32)
     local_sum = jnp.sum(hidden, axis=0)
     local_gram = jnp.dot(hidden.T, hidden, precision=lax.Precision.HIGHEST)
-    total_sum, total_gram = (by_axis(local_sum, GX_GY), by_axis(local_gram, GX_GY))
+    total_sum, total_gram = total_over_mesh(local_sum, local_gram)
     mean = total_sum / count
     sigma = total_gram / count - mean[:, None] * mean[None, :] + 1e-05 * ident
     return (mean, newton_whiten(sigma))

time: 149 us -> 105 us (0.70)
  blocking collectives: 101 us -> 0 us
  waiting for transfers between devices: 5.84 us -> 34.4 us
  starting transfers between devices: 13.8 us -> 38.3 us
  local copies, waits for them, and re-layouts: 8.91 us -> 11.6 us
    psum x4 -> x0, blocking collectives: 101 us -> none  [by_axis(): return functools.reduce(lax.psum, axes, value)]
    all_to_all x0 -> x2, waiting for transfers between devices: none -> 28.2 us  [exchange_sum(): return jnp.sum(lax.all_to_all(copies, axes, 0, 0, tiled=True), axis=0)]
    all_to_all x0 -> x2, starting transfers between devices: none -> 24.5 us  [exchange_sum(): return jnp.sum(lax.all_to_all(copies, axes, 0, 0, tiled=True), axis=0)]
    broadcast_in_dim x0 -> x2, local copies, waits for them, and re-layouts: none -> 1.91 us  [exchange_sum(): copies = jnp.broadcast_to(block[None], (count,) + block.shape)]
  transfers between devices with their start and end apart: 4 -> 6, of which waited for: 3 -> 5; matrix products, arithmetic and copies ran while one was open for 1% -> 1% of each run, Pallas kernels for 0% -> 0%
where the time goes in v1:
time: 105 us; the launch traced here: 104 us
  starting transfers between devices  38.3 us (36%)
  waiting for transfers between devices  34.4 us (33%)
  matrix products  15.1 us (14%)
  local copies, waits for them, and re-layouts  11.6 us (11%)
  other arithmetic  3.69 us (4%)
  between operations  1.17 us (1%)
    all_to_all x2, waiting for transfers between devices, exchange_sum(): return jnp.sum(lax.all_to_all(copies, axes, 0, 0, tiled=True), axis=0)  28.2 us
    all_to_all x2, starting transfers between devices, exchange_sum(): return jnp.sum(lax.all_to_all(copies, axes, 0, 0, tiled=True), axis=0)  24.5 us
    ppermute x2, starting transfers between devices, padded_2(): lax.ppermute(lax.slice_in_dim(block, block.shape[dim] - width, None, axis...  9.14 us
    dot_general x18, matrix products, convolve(): jnp.dot(tap, weights[first:first + 3 * width], preferred_element_type=jnp...  7.25 us
    ppermute x2, waiting for transfers between devices, padded_2(): lax.ppermute(lax.slice_in_dim(block, 0, width, axis=dim), axis, backward)  5.29 us
    ppermute x2, starting transfers between devices, padded_2(): lax.ppermute(lax.slice_in_dim(block, 0, width, axis=dim), axis, backward)  4.67 us
    dot_general x5, matrix products, newton_whiten(): jnp.dot(cube, normed, precision=lax.Precision.HIGHEST)  4.42 us
    slice x2, local copies, waits for them, and re-layouts, convolve(): tap = zcat[dx:dx + rows_x, dy:dy + rows_y].reshape(-1, 3 * width)  2.68 us
  transfers between devices with their start and end apart: 6, of which 5 were waited for; matrix products, arithmetic and copies ran while one was open for 1% of the time, Pallas kernels for 0%

profile of v1, /device:TPU:1, one launch (start us, length us, event | category | flops | bytes accessed | tf_op | source)
XLA Modules:
  0.0 104.2 jit_solution(10631039311655025600)
XLA Ops:
  0.0 4.0 %collective-permute-start = (bf16[2,8,4096]{2,1,0:T(8,128)(2,1)}, bf16[2,8,4096]{2,1,0:T(8,128)(2,1)S(1)}, u32[]{:S(2)}, u32[]{:S(2)}) collective-permute-start(bf16[2,8,4096]{2,1,0:T(8,128)(2,1)} %param.6), channel_id=1, source_target_pairs={{0,8},{8,16},{16,24},{24,32},{32,40},{40,48},{48,56},{56,64},{64,7... | collective-permute-start | bytes 393224 | tf_op jit(solution)/shard_map/ppermute | solution.py:19
  4.0 1.3 %collective-permute-start.1 = (bf16[2,8,4096]{2,1,0:T(8,128)(2,1)}, bf16[2,8,4096]{2,1,0:T(8,128)(2,1)S(1)}, u32[]{:S(2)}, u32[]{:S(2)}) collective-permute-start(bf16[2,8,4096]{2,1,0:T(8,128)(2,1)} %param.6), channel_id=1, source_target_pairs={{8,0},{16,8},{24,16},{32,24},{40,32},{48,40},{56,48},{64,56},{72,6... | collective-permute-start | bytes 393224 | tf_op jit(solution)/shard_map/ppermute | solution.py:22
  5.3 0.9 collective-permute-done
  6.3 0.9 constant_dynamic-update-slice_fusion.1
  7.2 2.8 %collective-permute-done.1 = bf16[2,8,4096]{2,1,0:T(8,128)(2,1)S(1)} collective-permute-done((bf16[2,8,4096]{2,1,0:T(8,128)(2,1)}, bf16[2,8,4096]{2,1,0:T(8,128)(2,1)S(1)}, u32[]{:S(2)}, u32[]{:S(2)}) %collective-permute-start.1) | collective-permute-done | bytes 131104 | tf_op jit(solution)/shard_map/ppermute | solution.py:22
  10.1 5.1 %collective-permute-start.2 = (bf16[6,2,4096]{2,1,0:T(2,128)(2,1)S(1)}, bf16[6,2,4096]{2,1,0:T(2,128)(2,1)S(1)}, u32[]{:S(2)}, u32[]{:S(2)}) collective-permute-start(bf16[6,2,4096]{2,1,0:T(2,128)(2,1)S(1)} %get-tuple-element.27), channel_id=1, source_target_pairs={{0,1},{1,2},{2,3},{3,4},{4,5},{5,6},{6,7},{8,9},{9,10},{10,11},{11... | collective-permute-start | bytes 294920 | tf_op jit(solution)/shard_map/ppermute | solution.py:19
  15.2 3.4 %collective-permute-start.3 = (bf16[6,2,4096]{2,1,0:T(2,128)(2,1)S(1)}, bf16[6,2,4096]{2,1,0:T(2,128)(2,1)S(1)}, u32[]{:S(2)}, u32[]{:S(2)}) collective-permute-start(bf16[6,2,4096]{2,1,0:T(2,128)(2,1)S(1)} %get-tuple-element.28), channel_id=1, source_target_pairs={{1,0},{2,1},{3,2},{4,3},{5,4},{6,5},{7,6},{9,8},{10,9},{11,10},{12... | collective-permute-start | bytes 294920 | tf_op jit(solution)/shard_map/ppermute | solution.py:22
  18.6 2.5 %collective-permute-done.3 = bf16[6,2,4096]{2,1,0:T(2,128)(2,1)S(1)} collective-permute-done((bf16[6,2,4096]{2,1,0:T(2,128)(2,1)S(1)}, bf16[6,2,4096]{2,1,0:T(2,128)(2,1)S(1)}, u32[]{:S(2)}, u32[]{:S(2)}) %collective-permute-start.3) | collective-permute-done | bytes 98336 | tf_op jit(solution)/shard_map/ppermute | solution.py:22
  21.5 1.2 %reshape.179 = bf16[6,12,64,64]{3,2,1,0:T(8,128)(2,1)S(1)} reshape(bf16[6,12,4096]{2,1,0:T(8,128)(2,1)S(1)} %pad_maximum_fusion.2) | data formatting | bytes 1179648 | tf_op jit(solution)/shard_map/reshape | solution.py:31
  22.8 1.0 pad_slice_fusion.1
  23.8 1.1 %pad_maximum_fusion = bf16[6,12,64,192]{3,2,1,0:T(8,128)(2,1)S(1)} fusion(bf16[6,12,64,64]{3,2,1,0:T(8,128)(2,1)S(1)} %get-tuple-element.24, bf16[6,12,64,64]{3,2,1,0:T(8,128)(2,1)S(1)} %reshape.179, bf16[6,12,64,64]{3,2,1,0:T(8,128)(2,1)S(1)} %get-tuple-element.23), kind=kLoop, calls=%fused_computation.11 | loop fusion | flops 5308416 | bytes 3538944 | tf_op jit(solution)/shard_map/concatenate | solution.py:33
  25.0 2.1 %fusion.37 = (bf16[4,10,64,192]{3,2,1,0:T(8,128)(2,1)S(1)}, bf16[4,10,64,192]{3,2,1,0:T(8,128)(2,1)S(1)}, bf16[4,10,64,192]{3,2,1,0:T(8,128)(2,1)S(1)}, bf16[4,1...) fusion(bf16[6,12,64,192]{3,2,1,0:T(8,128)(2,1)S(1)} %pad_maximu, ...), kind=kLoop, calls=%fused_computation.83 | loop fusion | bytes 17694720 | tf_op jit(solution)/shard_map/slice | solution.py:39
  27.6 0.5 convolution_add_fusion.7
  29.7 0.5 convolution_add_fusion.3
  30.8 0.5 convolution_add_fusion.1
  32.2 1.0 convolution_bitcast_fusion
  33.5 0.8 broadcast_in_dim.8
  34.3 16.3 %all-to-all-start = ((f32[16,33,1,128]{3,2,1,0:T(1,128)}), f32[16,33,1,128]{3,2,1,0:T(1,128)S(1)}, u32[]{:S(2)}, u32[]{:S(2)}) async-start(f32[16,33,1,128]{3,2,1,0:T(1,128)} %broadcast_in_dim.8), calls=%async_computation | async-start | bytes 540672 | tf_op jit(solution)/shard_map/all_to_all | solution.py:65
  51.1 16.7 %all-to-all-done = f32[16,33,1,128]{3,2,1,0:T(1,128)S(1)} async-done(((f32[16,33,1,128]{3,2,1,0:T(1,128)}), f32[16,33,1,128]{3,2,1,0:T(1,128)S(1)}, u32[]{:S(2)}, u32[]{:S(2)}) %all-to-all-start) | async-done | bytes 270368 | tf_op jit(solution)/shard_map/all_to_all | solution.py:65
  68.0 1.1 %broadcast_in_dim.9 = f32[32,33,1,128]{3,2,1,0:T(1,128)} broadcast(f32[33,128]{1,0:T(8,128)S(1)} %reduce_sum.40), dimensions={1,3} | broadcast | bytes 557568 | tf_op jit(solution)/shard_map/broadcast_in_dim | solution.py:64
  69.1 8.1 %all-to-all-start.1 = ((f32[32,33,1,128]{3,2,1,0:T(1,128)}), f32[32,33,1,128]{3,2,1,0:T(1,128)S(1)}, u32[]{:S(2)}, u32[]{:S(2)}) async-start(f32[32,33,1,128]{3,2,1,0:T(1,128)} %broadcast_in_dim.9), calls=%async_computation.1 | async-start | bytes 1081344 | tf_op jit(solution)/shard_map/all_to_all | solution.py:65
  77.5 11.5 %all-to-all-done.1 = f32[32,33,1,128]{3,2,1,0:T(1,128)S(1)} async-done(((f32[32,33,1,128]{3,2,1,0:T(1,128)}), f32[32,33,1,128]{3,2,1,0:T(1,128)S(1)}, u32[]{:S(2)}, u32[]{:S(2)}) %all-to-all-start.1) | async-done | bytes 540704 | tf_op jit(solution)/shard_map/all_to_all | solution.py:65
  89.7 0.6 select_reduce_fusion
  91.0 0.9 fusion.9
  92.3 0.9 fusion.8
  93.5 0.9 fusion.7
  94.7 0.9 fusion.6
  96.0 0.9 fusion.5
  96.9 0.8 fusion.1
  98.8 0.7 pad_maximum_fusion.1
  99.5 0.6 fusion.38
  103.3 0.9 reshape.202
  (66 shorter events, 11.4 us)
Async XLA Ops:
  0.0 6.3 %collective-permute-start = (bf16[2,8,4096]{2,1,0:T(8,128)(2,1)}, bf16[2,8,4096]{2,1,0:T(8,128)(2,1)S(1)}, u32[]{:S(2)}, u32[]{:S(2)}) collective-permute-start(bf16[2,8,4096]{2,1,0:T(8,128)(2,1)} %param.6), channel_id=1, source_target_pairs={{0,8},{8,16},{16,24},{24,32},{32,40},{40,48},{48,56},{56,64},{64,7... | collective-permute-start | bytes 393224 | tf_op jit(solution)/shard_map/ppermute | solution.py:19
  4.0 5.9 %collective-permute-start.1 = (bf16[2,8,4096]{2,1,0:T(8,128)(2,1)}, bf16[2,8,4096]{2,1,0:T(8,128)(2,1)S(1)}, u32[]{:S(2)}, u32[]{:S(2)}) collective-permute-start(bf16[2,8,4096]{2,1,0:T(8,128)(2,1)} %param.6), channel_id=1, source_target_pairs={{8,0},{16,8},{24,16},{32,24},{40,32},{48,40},{56,48},{64,56},{72,6... | collective-permute-start | bytes 393224 | tf_op jit(solution)/shard_map/ppermute | solution.py:22
  10.1 8.5 %collective-permute-start.2 = (bf16[6,2,4096]{2,1,0:T(2,128)(2,1)S(1)}, bf16[6,2,4096]{2,1,0:T(2,128)(2,1)S(1)}, u32[]{:S(2)}, u32[]{:S(2)}) collective-permute-start(bf16[6,2,4096]{2,1,0:T(2,128)(2,1)S(1)} %get-tuple-element.27), channel_id=1, source_target_pairs={{0,1},{1,2},{2,3},{3,4},{4,5},{5,6},{6,7},{8,9},{9,10},{10,11},{11... | collective-permute-start | bytes 294920 | tf_op jit(solution)/shard_map/ppermute | solution.py:19
  15.2 5.9 %collective-permute-start.3 = (bf16[6,2,4096]{2,1,0:T(2,128)(2,1)S(1)}, bf16[6,2,4096]{2,1,0:T(2,128)(2,1)S(1)}, u32[]{:S(2)}, u32[]{:S(2)}) collective-permute-start(bf16[6,2,4096]{2,1,0:T(2,128)(2,1)S(1)} %get-tuple-element.28), channel_id=1, source_target_pairs={{1,0},{2,1},{3,2},{4,3},{5,4},{6,5},{7,6},{9,8},{10,9},{11,10},{12... | collective-permute-start | bytes 294920 | tf_op jit(solution)/shard_map/ppermute | solution.py:22
  25.0 2.1 %copy-start.1 = (bf16[1728,64]{0,1:T(8,128)(2,1)S(1)}, bf16[1728,64]{0,1:T(8,128)(2,1)}, u32[]{:S(2)}) copy-start(bf16[1728,64]{0,1:T(8,128)(2,1)} %param.7) | copy-start | bytes 663556
  34.3 33.5 %all-to-all-start = ((f32[16,33,1,128]{3,2,1,0:T(1,128)}), f32[16,33,1,128]{3,2,1,0:T(1,128)S(1)}, u32[]{:S(2)}, u32[]{:S(2)}) async-start(f32[16,33,1,128]{3,2,1,0:T(1,128)} %broadcast_in_dim.8), calls=%async_computation | async-start | bytes 540672 | tf_op jit(solution)/shard_map/all_to_all | solution.py:65
  69.1 19.8 %all-to-all-start.1 = ((f32[32,33,1,128]{3,2,1,0:T(1,128)}), f32[32,33,1,128]{3,2,1,0:T(1,128)S(1)}, u32[]{:S(2)}, u32[]{:S(2)}) async-start(f32[32,33,1,128]{3,2,1,0:T(1,128)} %broadcast_in_dim.9), calls=%async_computation.1 | async-start | bytes 1081344 | tf_op jit(solution)/shard_map/all_to_all | solution.py:65
  77.5 19.4 %copy-start.3 = (f32[64]{0:T(128)S(1)}, f32[64]{0:T(128)}, u32[]{:S(2)}) copy-start(f32[64]{0:T(128)} %param.9) | copy-start | bytes 772
  77.5 19.4 %copy-start.4 = (f32[64]{0:T(128)S(1)}, f32[64]{0:T(128)}, u32[]{:S(2)}) copy-start(f32[64]{0:T(128)} %param.8) | copy-start | bytes 772
  99.5 0.9 copy-start
  102.2 0.7 copy-start.2

commit v2 on v0

v2 whole, which is shorter than its diff:
```python
import functools

import jax
import jax.numpy as jnp
from jax import lax
from jax.experimental import pallas as pl
from jax.experimental.pallas import tpu as pltpu
from jax.sharding import Mesh
from jax.sharding import PartitionSpec as P

NEWTON = 5
GX = ("gx_0", "gx_1")
GY = ("gy_0", "gy_1")
PACK = 4
F32 = jnp.float32
BF16 = jnp.bfloat16
HIGHEST = lax.Precision.HIGHEST
PAY = 17


def params():
    return pltpu.CompilerParams(vmem_limit_bytes=48 * 1024 * 1024)


def shift_exchange(low_edge, high_edge, axis):
    count = lax.axis_size(axis)
    forward = [(i, i + 1) for i in range(count - 1)]
    backward = [(target, source) for source, target in forward]
    return lax.ppermute(high_edge, axis, forward), lax.ppermute(low_edge, axis, backward)


def rows_kernel(v_ref, o_ref, f_ref):
    slabs, sub, merged = v_ref.shape
    rows, lanes = o_ref.shape[2:]
    for x in range(slabs):
        for b in range(rows):
            for h in range(lanes // 128):
                first = b * lanes + h * 128
                f_ref[h, pl.ds(x * sub * rows + b, sub, stride=rows), :] = v_ref[
                    x, :, first : first + 128
                ].astype(F32)
    for h in range(lanes // 128):
        o_ref[:, :, :, h * 128 : (h + 1) * 128] = f_ref[h].astype(BF16).reshape(slabs, sub, rows, 128)


def band_kernel(w_ref, o_ref):
    c = w_ref.shape[0]
    o_ref[...] = jnp.zeros_like(o_ref)
    for t in range(9):
        w = w_ref[:, t * 3 * c : (t + 1) * 3 * c]
        base = t * 6 * c
        o_ref[0:c, base : base + 2 * c] = w[:, c:]
        o_ref[0:c, base + 5 * c : base + 6 * c] = w[:, :c]
        for k in range(1, PACK):
            first = base + (k - 1) * c
            o_ref[k * c : (k + 1) * c, first : first + 3 * c] = w


def widen(f_ref, x_ref):
    rows = x_ref.shape[2]
    x_ref[:, :, :, 0:256] = f_ref[:, :, 8 : 8 + rows, :].astype(BF16)
    after = f_ref[:, :, 9 : 9 + rows, 0:128]
    before = f_ref[:, :, 7 : 7 + rows, 128:256]
    lane = lax.broadcasted_iota(jnp.int32, after.shape, 3)
    x_ref[:, :, :, 256:384] = jnp.where(lane < 64, after, before).astype(BF16)


def clear_ends(f_ref, rows):
    cells_x, cells_y, _, lanes = f_ref.shape
    zero = jnp.zeros((cells_x, cells_y, 8, lanes), F32)
    f_ref[:, :, 0:8, :] = zero
    f_ref[:, :, 8 + rows : 16 + rows, :] = zero


def banded_conv(x_ref, w_ref):
    nx, ny, rows, k = x_ref.shape
    nx, ny = nx - 2, ny - 2
    acc = None
    for dx in range(3):
        taps = [x_ref[dx : dx + nx, dy : dy + ny].reshape(nx * ny * rows, k) for dy in range(3)]
        part = lax.dot_general(
            jnp.concatenate(taps, axis=1),
            w_ref[:, dx * 3 * k : (dx + 1) * 3 * k],
            (((1,), (1,)), ((), ())),
            preferred_element_type=F32,
        )
        acc = part if acc is None else acc + part
    return acc


def square_iota(n):
    return lax.broadcasted_iota(jnp.int32, (n, n), 0), lax.broadcasted_iota(jnp.int32, (n, n), 1)


def hidden_kernel(own_ref, xlo_ref, xhi_ref, ylo_ref, yhi_ref, w_ref, hidden_ref, pay_ref, f_ref, x_ref):
    rows = own_ref.shape[2]
    cx, cy = own_ref.shape[:2]
    clear_ends(f_ref, rows)
    f_ref[:, 0:2, 8 : 8 + rows, :] = ylo_ref[...].astype(F32)
    f_ref[0:2, 2 : 2 + cy, 8 : 8 + rows, :] = xlo_ref[...].astype(F32)
    f_ref[2 : 2 + cx, 2 : 2 + cy, 8 : 8 + rows, :] = own_ref[...].astype(F32)
    f_ref[2 + cx : 4 + cx, 2 : 2 + cy, 8 : 8 + rows, :] = xhi_ref[...].astype(F32)
    f_ref[:, 2 + cy : 4 + cy, 8 : 8 + rows, :] = yhi_ref[...].astype(F32)
    widen(f_ref, x_ref)
    hidden_ref[...] = banded_conv(x_ref, w_ref).reshape(hidden_ref.shape)
    own = hidden_ref[1 : 1 + cx, 1 : 1 + cy].reshape(cx * cy * rows, 256)
    wide = lax.dot_general(own, own, (((0,), (0,)), ((), ())), precision=HIGHEST, preferred_element_type=F32)
    sums = jnp.sum(own, axis=0, keepdims=True)
    gram = wide[0:64, 0:64]
    total = sums[:, 0:64]
    for k in range(1, PACK):
        gram = gram + wide[k * 64 : (k + 1) * 64, k * 64 : (k + 1) * 64]
        total = total + sums[:, k * 64 : (k + 1) * 64]
    i, j = square_iota(32)
    low = gram[32:, 32:]
    tri = jnp.where(j >= i, gram[:32, :32], low)
    cross = gram[:32, 32:]
    block = jnp.concatenate([tri[:16], tri[16:], cross[:16], cross[16:]], axis=1)
    diag = jnp.sum(jnp.where(i == j, low, 0.0), axis=0, keepdims=True)
    last = jnp.concatenate([diag, total, jnp.zeros((1, 32), F32)], axis=1)
    for p in range(pay_ref.shape[0]):
        for r in range(16):
            pay_ref[p, r] = block[r : r + 1]
        pay_ref[p, 16] = last


def relay_kernel(in_ref, out_ref):
    total = jnp.sum(in_ref[...], axis=0)
    for p in range(out_ref.shape[0]):
        out_ref[p] = total


def transposed(a):
    return jnp.transpose(a)


def moments(pay_ref, p_ref, count):
    total = jnp.sum(pay_ref[...], axis=0)
    for r in range(PAY):
        p_ref[r : r + 1, :] = total[r]
    block = p_ref[0:16, :]
    last = p_ref[16:17, :]
    i, j = square_iota(32)
    tri = jnp.concatenate([block[:, 0:32], block[:, 32:64]], axis=0)
    cross = jnp.concatenate([block[:, 64:96], block[:, 96:128]], axis=0)
    flip = transposed(tri)
    top = jnp.where(j >= i, tri, flip)
    low = jnp.where(j < i, tri, flip)
    low = jnp.where(i == j, jnp.broadcast_to(last[:, 0:32], (32, 32)), low)
    gram = jnp.concatenate(
        [
            jnp.concatenate([top, cross], axis=1),
            jnp.concatenate([transposed(cross), low], axis=1),
        ],
        axis=0,
    )
    mean = last[:, 32:96] / count
    i, j = square_iota(64)
    eye = jnp.where(i == j, 1.0, 0.0).astype(F32)
    column = jnp.sum(eye * mean, axis=1, keepdims=True)
    return mean, gram / count - column * mean + 1e-05 * eye, eye


def newton_whiten(sigma, eye):
    dot = functools.partial(jnp.dot, precision=HIGHEST, preferred_element_type=F32)
    trace = jnp.sum(jnp.sum(sigma * eye, axis=1, keepdims=True), axis=0, keepdims=True)
    normed = sigma / trace
    proj = 1.5 * eye - 0.5 * normed
    for _ in range(NEWTON - 1):
        both = dot(proj, jnp.concatenate([proj, normed], axis=1))
        proj = 1.5 * proj - 0.5 * dot(both[:, 0:64], both[:, 64:128])
    return proj / jnp.sqrt(trace)


def output_kernel(
    inside_ref, pay_ref, hidden_ref, gain_ref, shift_ref, w_ref, bias_ref, out_ref, p_ref, f_ref, x_ref, o_ref, *, count
):
    nx, ny, rows, lanes = hidden_ref.shape
    mean, sigma, eye = moments(pay_ref, p_ref, count)
    whiten = newton_whiten(sigma, eye)
    i, j = square_iota(lanes)
    wide = jnp.concatenate([whiten] * PACK, axis=1)
    wide = jnp.concatenate([wide] * PACK, axis=0)
    wide = jnp.where(i >> 6 == j >> 6, wide, 0.0)
    mean = jnp.concatenate([mean] * PACK, axis=1)
    gain = jnp.concatenate([gain_ref[...]] * PACK, axis=1)
    shift = jnp.concatenate([shift_ref[...]] * PACK, axis=1)
    centered = hidden_ref[...].reshape(nx * ny * rows, lanes) - mean
    normalized = jnp.dot(centered, wide, precision=HIGHEST, preferred_element_type=F32)
    act = jnp.maximum(gain * normalized + shift, 0.0).reshape(hidden_ref.shape)
    clear_ends(f_ref, rows)
    f_ref[:, :, 8 : 8 + rows, :] = act
    for flag, edge in ((0, f_ref.at[0]), (1, f_ref.at[nx - 1]), (2, f_ref.at[:, 0]), (3, f_ref.at[:, ny - 1])):

        @pl.when(inside_ref[flag] == 0)
        def _(edge=edge):
            edge[...] = jnp.zeros_like(edge)

    widen(f_ref, x_ref)
    bias = jnp.concatenate([bias_ref[...]] * PACK, axis=1)
    result = banded_conv(x_ref, w_ref) + bias
    for h in range(lanes // 128):
        o_ref[h] = result[:, h * 128 : (h + 1) * 128]
    slabs, sub, _ = out_ref.shape
    for x in range(slabs):
        for b in range(rows):
            for h in range(lanes // 128):
                first = b * lanes + h * 128
                out_ref[x, :, first : first + 128] = o_ref[
                    h, pl.ds(x * sub * rows + b, sub, stride=rows), :
                ].astype(BF16)


def exchange(block, axes):
    return lax.all_to_all(block, axes, 0, 0, tiled=True)


def group_size(axes):
    return functools.reduce(lambda total, axis: total * lax.axis_size(axis), axes, 1)


def local(volume, conv_first, gain, shift, conv_second, bias_second):
    width = bias_second.shape[0]
    cx, cy, merged = volume.shape
    lanes = PACK * width
    rows = merged // lanes
    count = float(cx * group_size(GX) * cy * group_size(GY) * (merged // width))
    call = functools.partial(pl.pallas_call, compiler_params=params())
    own = call(
        rows_kernel,
        out_shape=jax.ShapeDtypeStruct((cx, cy, rows, lanes), BF16),
        scratch_shapes=[pltpu.VMEM((lanes // 128, cx * cy * rows, 128), F32)],
        name="rows",
    )(volume)
    band = call(band_kernel, out_shape=jax.ShapeDtypeStruct((lanes, 54 * width), BF16), name="band")
    first, second = band(conv_first.T), band(conv_second.T)
    xlo, xhi = shift_exchange(own[:2], own[cx - 2 :], GX)
    sides = jnp.concatenate([xlo, own, xhi], axis=0)
    ylo, yhi = shift_exchange(sides[:, :2], sides[:, cy - 2 :], GY)
    hidden, pay = call(
        hidden_kernel,
        out_shape=(
            jax.ShapeDtypeStruct((cx + 2, cy + 2, rows, lanes), F32),
            jax.ShapeDtypeStruct((group_size(GX[:1]), PAY, 1, 128), F32),
        ),
        scratch_shapes=[
            pltpu.VMEM((cx + 4, cy + 4, rows + 16, lanes), F32),
            pltpu.VMEM((cx + 4, cy + 4, rows, 6 * width), BF16),
        ],
        name="hidden",
    )(own, xlo, xhi, ylo, yhi, first)
    rest = GX[1:] + GY
    pay = exchange(pay, GX[:1])
    pay = call(
        relay_kernel, out_shape=jax.ShapeDtypeStruct((group_size(rest), PAY, 1, 128), F32), name="relay"
    )(pay)
    pay = exchange(pay, rest)
    at_x, at_y = lax.axis_index(GX), lax.axis_index(GY)
    inside = jnp.stack([at_x > 0, at_x < group_size(GX) - 1, at_y > 0, at_y < group_size(GY) - 1]).astype(jnp.int32)
    in_vmem = pl.BlockSpec(memory_space=pltpu.VMEM)
    return call(
        functools.partial(output_kernel, count=count),
        out_shape=jax.ShapeDtypeStruct((cx, cy, merged), BF16),
        in_specs=[pl.BlockSpec(memory_space=pltpu.SMEM)] + [in_vmem] * 6,
        out_specs=in_vmem,
        scratch_shapes=[
            pltpu.VMEM((24, 128), F32),
            pltpu.VMEM((cx + 2, cy + 2, rows + 16, lanes), F32),
            pltpu.VMEM((cx + 2, cy + 2, rows, 6 * width), BF16),
            pltpu.VMEM((lanes // 128, cx * cy * rows, 128), F32),
        ],
        name="output",
    )(inside, pay, hidden, gain[None], shift[None], second, bias_second[None])


def solution(mesh):
    torus = Mesh(mesh.devices.reshape(16, 4, 4, 2), GX + GY)
    placed = (P(GX, GY, None), P(), P(), P(), P(), P())
    return jax.shard_map(
        local, mesh=torus, in_specs=placed, out_specs=P(GX, GY, None), check_vma=False
    )
```

time: 149 us -> 77.5 us (0.52)
  blocking collectives: 101 us -> 29.3 us
  matrix products: 15.1 us -> 0 us
  Pallas kernels: 0 us -> 10 us
  waiting for transfers between devices: 5.84 us -> 14.5 us
  starting transfers between devices: 13.8 us -> 21.3 us
  local copies, waits for them, and re-layouts: 8.91 us -> 1.86 us
  other arithmetic: 3.24 us -> 0.1 us
    psum x4 -> x0, blocking collectives: 101 us -> none  [by_axis(): return functools.reduce(lax.psum, axes, value)]
    all_to_all x0 -> x1, blocking collectives: none -> 29.3 us  [exchange(): return lax.all_to_all(block, axes, 0, 0, tiled=True)]
    dot_general x35 -> x0, matrix products: 15.1 us -> none  [the longest x18 7.25 us: convolve(): jnp.dot(tap, weights[first:first + 3 * width], preferred_element_type=jnp...]
    pallas_call x0 -> x6, Pallas kernels: none -> 10 us  [the longest x1 5.95 us: local(): call(functools.partial(output_kernel, count=count), out_shape=jax.ShapeDt...]
    all_to_all x0 -> x1, waiting for transfers between devices: none -> 8.72 us  [exchange(): return lax.all_to_all(block, axes, 0, 0, tiled=True)]
    all_to_all x0 -> x1, starting transfers between devices: none -> 7.45 us  [exchange(): return lax.all_to_all(block, axes, 0, 0, tiled=True)]
    slice x5 -> x0, local copies, waits for them, and re-layouts: 4.4 us -> none  [the longest x2 2.68 us: convolve(): tap = zcat[dx:dx + rows_x, dy:dy + rows_y].reshape(-1, 3 * width)]
    reshape x2 -> x0, local copies, waits for them, and re-layouts: 2.18 us -> none  [the longest x1 1.25 us: convolve(): vol = padded.reshape(rows_x + 2, rows_y + 2, depth, width)]
  transfers between devices with their start and end apart: 4 -> 5, of which waited for: 3 -> 4; matrix products, arithmetic and copies ran while one was open for 1% -> 0% of each run, Pallas kernels for 0% -> 1%
where the time goes in v2:
time: 77.5 us; the launch traced here: 77.2 us
  blocking collectives  29.3 us (38%)
  starting transfers between devices  21.3 us (27%)
  waiting for transfers between devices  14.5 us (19%)
  Pallas kernels  10 us (13%)
  local copies, waits for them, and re-layouts  1.86 us (2%)
    all_to_all x1, blocking collectives, exchange(): return lax.all_to_all(block, axes, 0, 0, tiled=True)  29.3 us
    ppermute x2, starting transfers between devices, shift_exchange(): lax.ppermute(high_edge, axis, forward)  9.15 us
    all_to_all x1, waiting for transfers between devices, exchange(): return lax.all_to_all(block, axes, 0, 0, tiled=True)  8.72 us
    all_to_all x1, starting transfers between devices, exchange(): return lax.all_to_all(block, axes, 0, 0, tiled=True)  7.45 us
    pallas_call x1, Pallas kernels, local(): call(functools.partial(output_kernel, count=count), out_shape=jax.ShapeDt...  5.95 us
    ppermute x2, waiting for transfers between devices, shift_exchange(): lax.ppermute(low_edge, axis, backward)  5.14 us
    ppermute x2, starting transfers between devices, shift_exchange(): lax.ppermute(low_edge, axis, backward)  4.67 us
    pallas_call x1, Pallas kernels, local(): call(hidden_kernel, out_shape=(jax.ShapeDtypeStruct((cx + 2, cy + 2, rows...  2.59 us
  transfers between devices with their start and end apart: 5, of which 4 were waited for; matrix products, arithmetic and copies ran while one was open for 0% of the time, Pallas kernels for 1%

profile of v2, /device:TPU:1, one launch (start us, length us, event | category | flops | bytes accessed | tf_op | source)
XLA Modules:
  0.0 77.2 jit_solution(13174480484674464834)
XLA Ops:
  0.0 0.0 copy-start.2
  0.0 0.9 %copy-done.2 = bf16[2,8,4096]{2,1,0:T(8,128)(2,1)S(1)} copy-done((bf16[2,8,4096]{2,1,0:T(8,128)(2,1)S(1)}, bf16[2,8,4096]{2,1,0:T(8,128)(2,1)}, u32[]{:S(2)}) %copy-start.2) | copy-done | bytes 131096
  0.9 0.1 rows.1.own_ref
  1.0 4.0 %collective-permute-start = (bf16[2,8,16,256]{3,2,1,0:T(8,128)(2,1)S(1)}, bf16[2,8,16,256]{3,2,1,0:T(8,128)(2,1)S(1)}, u32[]{:S(2)}, u32[]{:S(2)}) collective-permute-start(bf16[2,8,16,256]{3,2,1,0:T(8,128)(2,1)S(1)} %rows.1.own_ref), channel_id=1, source_target_pairs={{0,8},{8,16},{16,24},{24,32},{32,40},{40,48},{48,56},{56,64},{64,7... | collective-permute-start | bytes 393224 | tf_op jit(solution)/shard_map/ppermute | solution.py:29
  5.1 1.3 %collective-permute-start.1 = (bf16[2,8,16,256]{3,2,1,0:T(8,128)(2,1)S(1)}, bf16[2,8,16,256]{3,2,1,0:T(8,128)(2,1)S(1)}, u32[]{:S(2)}, u32[]{:S(2)}) collective-permute-start(bf16[2,8,16,256]{3,2,1,0:T(8,128)(2,1)S(1)} %rows.1.own_ref), channel_id=1, source_target_pairs={{8,0},{16,8},{24,16},{32,24},{40,32},{48,40},{56,48},{64,56},{72,6... | collective-permute-start | bytes 393224 | tf_op jit(solution)/shard_map/ppermute | solution.py:29
  6.4 0.6 collective-permute-done.xlo_ref
  7.0 3.8 %collective-permute-done.1.xhi_ref = bf16[2,8,16,256]{3,2,1,0:T(8,128)(2,1)S(1)} collective-permute-done((bf16[2,8,16,256]{3,2,1,0:T(8,128)(2,1)S(1)}, bf16[2,8,16,256]{3,2,1,0:T(8,128)(2,1)S(1)}, u32[]{:S(2)}, u32[]{:S(2)}) %collective-permute-start.1) | collective-permute-done | bytes 131104 | tf_op jit(solution)/shard_map/ppermute | solution.py:29
  10.8 5.1 %collective-permute-start.2 = (bf16[6,2,16,256]{3,2,1,0:T(8,128)(2,1)S(1)}, bf16[6,2,16,256]{3,2,1,0:T(8,128)(2,1)S(1)}, u32[]{:S(2)}, u32[]{:S(2)}) collective-permute-start(bf16[6,2,16,256]{3,2,1,0:T(8,128)(2,1)S(1)} %get-tuple-element.10), channel_id=1, source_target_pairs={{0,1},{1,2},{2,3},{3,4},{4,5},{5,6},{6,7},{8,9},{9,10},{10,11},{11... | collective-permute-start | bytes 294920 | tf_op jit(solution)/shard_map/ppermute | solution.py:29
  15.9 3.4 %collective-permute-start.3 = (bf16[6,2,16,256]{3,2,1,0:T(8,128)(2,1)S(1)}, bf16[6,2,16,256]{3,2,1,0:T(8,128)(2,1)S(1)}, u32[]{:S(2)}, u32[]{:S(2)}) collective-permute-start(bf16[6,2,16,256]{3,2,1,0:T(8,128)(2,1)S(1)} %get-tuple-element.9), channel_id=1, source_target_pairs={{1,0},{2,1},{3,2},{4,3},{5,4},{6,5},{7,6},{9,8},{10,9},{11,10},{12... | collective-permute-start | bytes 294920 | tf_op jit(solution)/shard_map/ppermute | solution.py:29
  19.3 0.0 copy-start
  19.3 0.9 %copy-done = bf16[1728,64]{0,1:T(8,128)(2,1)S(1)} copy-done((bf16[1728,64]{0,1:T(8,128)(2,1)S(1)}, bf16[1728,64]{0,1:T(8,128)(2,1)}, u32[]{:S(2)}) %copy-start) | copy-done | bytes 221208
  20.2 0.2 band.2.w_ref
  20.5 0.0 copy-start.1
  20.5 0.0 collective-permute-done.2.ylo_ref
  20.5 1.3 %collective-permute-done.3.yhi_ref = bf16[6,2,16,256]{3,2,1,0:T(8,128)(2,1)S(1)} collective-permute-done((bf16[6,2,16,256]{3,2,1,0:T(8,128)(2,1)S(1)}, bf16[6,2,16,256]{3,2,1,0:T(8,128)(2,1)S(1)}, u32[]{:S(2)}, u32[]{:S(2)}) %collective-permute-start.3) | collective-permute-done | bytes 98336 | tf_op jit(solution)/shard_map/ppermute | solution.py:29
  21.8 2.6 %hidden.1 = (f32[4,10,16,256]{3,2,1,0:T(8,128)S(1)}, f32[16,17,1,128]{3,2,1,0:T(1,128)S(1)}) custom-call(bf16[2,8,16,256]{3,2,1,0:T(8,128)(2,1)S(1)} %rows.1.own_ref, bf16[2,8,16,256]{3,2,1,0:T(8,128)(2,1)S(1)} %collective-permute-done.xlo_ref, bf16[2,8,16,256]{3,2,1,0:T(8,128)(2,1)S(1)} %collective-permute-done.1.xhi_ref, ...), custom_call_target="tpu_custom_call" | custom-call | tf_op jit(solution)/shard_map/hidden/pallas_call | solution.py:240
  24.4 0.0 copy-start.3
  24.5 0.0 copy-start.4
  24.5 0.0 copy-start.5
  24.5 29.3 %all_to_all.10.in_ref = f32[16,17,1,128]{3,2,1,0:T(1,128)S(1)} all-to-all(f32[16,17,1,128]{3,2,1,0:T(1,128)S(1)} %get-tuple-element.7), channel_id=1, replica_groups=mesh['gx_0'=16,'gx_1'=4,'gy_0'=4,'gy_1'=2] {'gx_0'}, dimensions={0} | all-to-all | bytes 278528 | tf_op jit(solution)/shard_map/all_to_all | solution.py:215
  53.8 0.9 %relay.1 = f32[32,17,1,128]{3,2,1,0:T(1,128)} custom-call(f32[16,17,1,128]{3,2,1,0:T(1,128)S(1)} %all_to_all.10.in_ref), custom_call_target="tpu_custom_call" | custom-call | tf_op jit(solution)/shard_map/relay/pallas_call | solution.py:254
  54.7 7.5 %all-to-all-start.1 = ((f32[32,17,1,128]{3,2,1,0:T(1,128)}), f32[32,17,1,128]{3,2,1,0:T(1,128)S(1)}, u32[]{:S(2)}, u32[]{:S(2)}) async-start(f32[32,17,1,128]{3,2,1,0:T(1,128)} %relay.1), calls=%async_computation.1 | async-start | bytes 557056 | tf_op jit(solution)/shard_map/all_to_all | solution.py:215
  62.2 0.0 copy-done.1
  62.2 0.2 band.3.w_ref
  62.4 0.1 add_convert_fusion.inside_ref
  62.5 8.7 %all-to-all-done.1.pay_ref = f32[32,17,1,128]{3,2,1,0:T(1,128)S(1)} async-done(((f32[32,17,1,128]{3,2,1,0:T(1,128)}), f32[32,17,1,128]{3,2,1,0:T(1,128)S(1)}, u32[]{:S(2)}, u32[]{:S(2)}) %all-to-all-start.1) | async-done | bytes 278560 | tf_op jit(solution)/shard_map/all_to_all | solution.py:215
  71.2 0.0 copy-done.3
  71.2 0.0 copy-done.4
  71.2 0.0 copy-done.5
  71.2 6.0 %output.1 = bf16[2,8,4096]{2,1,0:T(8,128)(2,1)} custom-call(s32[4]{0:T(128)S(1)} %add_convert_fusion.inside_ref, f32[32,17,1,128]{3,2,1,0:T(1,128)S(1)} %all-to-all-done.1.pay_ref, f32[4,10,16,256]{3,2,1,0:T(8,128)S(1)} %get-tuple-element.8.hidden_ref, f32[1,64]{1,0:T(1,128)S(1)} %bitcast.11, f32[1,64]{1,0:T(1,128)S(1)} %bitcast.12, ...), custom_call_target="tpu_custom_call" | custom-call | tf_op jit(solution)/shard_map/output/pallas_call | solution.py:261
  (1 shorter events, 0.0 us)
Async XLA Ops:
  0.0 0.9 %copy-start.2 = (bf16[2,8,4096]{2,1,0:T(8,128)(2,1)S(1)}, bf16[2,8,4096]{2,1,0:T(8,128)(2,1)}, u32[]{:S(2)}) copy-start(bf16[2,8,4096]{2,1,0:T(8,128)(2,1)} %v_ref.1) | copy-start | bytes 393220
  1.0 6.0 %collective-permute-start = (bf16[2,8,16,256]{3,2,1,0:T(8,128)(2,1)S(1)}, bf16[2,8,16,256]{3,2,1,0:T(8,128)(2,1)S(1)}, u32[]{:S(2)}, u32[]{:S(2)}) collective-permute-start(bf16[2,8,16,256]{3,2,1,0:T(8,128)(2,1)S(1)} %rows.1.own_ref), channel_id=1, source_target_pairs={{0,8},{8,16},{16,24},{24,32},{32,40},{40,48},{48,56},{56,64},{64,7... | collective-permute-start | bytes 393224 | tf_op jit(solution)/shard_map/ppermute | solution.py:29
  5.1 5.7 %collective-permute-start.1 = (bf16[2,8,16,256]{3,2,1,0:T(8,128)(2,1)S(1)}, bf16[2,8,16,256]{3,2,1,0:T(8,128)(2,1)S(1)}, u32[]{:S(2)}, u32[]{:S(2)}) collective-permute-start(bf16[2,8,16,256]{3,2,1,0:T(8,128)(2,1)S(1)} %rows.1.own_ref), channel_id=1, source_target_pairs={{8,0},{16,8},{24,16},{32,24},{40,32},{48,40},{56,48},{64,56},{72,6... | collective-permute-start | bytes 393224 | tf_op jit(solution)/shard_map/ppermute | solution.py:29
  10.8 9.7 %collective-permute-start.2 = (bf16[6,2,16,256]{3,2,1,0:T(8,128)(2,1)S(1)}, bf16[6,2,16,256]{3,2,1,0:T(8,128)(2,1)S(1)}, u32[]{:S(2)}, u32[]{:S(2)}) collective-permute-start(bf16[6,2,16,256]{3,2,1,0:T(8,128)(2,1)S(1)} %get-tuple-element.10), channel_id=1, source_target_pairs={{0,1},{1,2},{2,3},{3,4},{4,5},{5,6},{6,7},{8,9},{9,10},{10,11},{11... | collective-permute-start | bytes 294920 | tf_op jit(solution)/shard_map/ppermute | solution.py:29
  15.9 5.9 %collective-permute-start.3 = (bf16[6,2,16,256]{3,2,1,0:T(8,128)(2,1)S(1)}, bf16[6,2,16,256]{3,2,1,0:T(8,128)(2,1)S(1)}, u32[]{:S(2)}, u32[]{:S(2)}) collective-permute-start(bf16[6,2,16,256]{3,2,1,0:T(8,128)(2,1)S(1)} %get-tuple-element.9), channel_id=1, source_target_pairs={{1,0},{2,1},{3,2},{4,3},{5,4},{6,5},{7,6},{9,8},{10,9},{11,10},{12... | collective-permute-start | bytes 294920 | tf_op jit(solution)/shard_map/ppermute | solution.py:29
  19.3 0.9 %copy-start = (bf16[1728,64]{0,1:T(8,128)(2,1)S(1)}, bf16[1728,64]{0,1:T(8,128)(2,1)}, u32[]{:S(2)}) copy-start(bf16[1728,64]{0,1:T(8,128)(2,1)} %param.7) | copy-start | bytes 663556
  20.5 41.7 %copy-start.1 = (bf16[1728,64]{0,1:T(8,128)(2,1)S(1)}, bf16[1728,64]{0,1:T(8,128)(2,1)}, u32[]{:S(2)}) copy-start(bf16[1728,64]{0,1:T(8,128)(2,1)} %param.10) | copy-start | bytes 663556
  24.4 46.8 %copy-start.3 = (f32[64]{0:T(128)S(1)}, f32[64]{0:T(128)}, u32[]{:S(2)}) copy-start(f32[64]{0:T(128)} %param.8) | copy-start | bytes 772
  24.5 46.8 %copy-start.4 = (f32[64]{0:T(128)S(1)}, f32[64]{0:T(128)}, u32[]{:S(2)}) copy-start(f32[64]{0:T(128)} %param.9) | copy-start | bytes 772
  24.5 46.8 %copy-start.5 = (f32[64]{0:T(128)S(1)}, f32[64]{0:T(128)}, u32[]{:S(2)}) copy-start(f32[64]{0:T(128)} %param.11) | copy-start | bytes 772
  54.7 16.5 %all-to-all-start.1 = ((f32[32,17,1,128]{3,2,1,0:T(1,128)}), f32[32,17,1,128]{3,2,1,0:T(1,128)S(1)}, u32[]{:S(2)}, u32[]{:S(2)}) async-start(f32[32,17,1,128]{3,2,1,0:T(1,128)} %relay.1), calls=%async_computation.1 | async-start | bytes 557056 | tf_op jit(solution)/shard_map/all_to_all | solution.py:215

commit v3 on v2

--- a/solution.py
+++ b/solution.py
@@ -250,13 +250,14 @@
         name="hidden",
     )(own, xlo, xhi, ylo, yhi, first)
     rest = GX[1:] + GY
+    at_x, at_y = lax.axis_index(GX), lax.axis_index(GY)
+    inside = jnp.stack([at_x > 0, at_x < group_size(GX) - 1, at_y > 0, at_y < group_size(GY) - 1]).astype(jnp.int32)
+    pay, second, inside = lax.optimization_barrier((pay, second, inside))
     pay = exchange(pay, GX[:1])
     pay = call(
         relay_kernel, out_shape=jax.ShapeDtypeStruct((group_size(rest), PAY, 1, 128), F32), name="relay"
     )(pay)
     pay = exchange(pay, rest)
-    at_x, at_y = lax.axis_index(GX), lax.axis_index(GY)
-    inside = jnp.stack([at_x > 0, at_x < group_size(GX) - 1, at_y > 0, at_y < group_size(GY) - 1]).astype(jnp.int32)
     in_vmem = pl.BlockSpec(memory_space=pltpu.VMEM)
     return call(
         functools.partial(output_kernel, count=count),

time: 77.5 us -> 76.5 us (0.987)
  blocking collectives: 29.3 us -> 45.5 us
  waiting for transfers between devices: 14.5 us -> 5.42 us
  starting transfers between devices: 21.3 us -> 13.8 us
    all_to_all x1 -> x2, blocking collectives: 29.3 us -> 45.5 us  [exchange(): return lax.all_to_all(block, axes, 0, 0, tiled=True)]
    all_to_all x1 -> x0, waiting for transfers between devices: 8.72 us -> none  [exchange(): return lax.all_to_all(block, axes, 0, 0, tiled=True)]
    all_to_all x1 -> x0, starting transfers between devices: 7.45 us -> none  [exchange(): return lax.all_to_all(block, axes, 0, 0, tiled=True)]
  transfers between devices with their start and end apart: 5 -> 4, of which waited for: 4 -> 2; matrix products, arithmetic and copies ran while one was open for 0% -> 0% of each run, Pallas kernels for 1% -> 1%
where the time goes in v3:
time: 76.5 us; the launch traced here: 76.2 us
  blocking collectives  45.5 us (59%)
  starting transfers between devices  13.8 us (18%)
  Pallas kernels  9.29 us (12%)
  waiting for transfers between devices  5.42 us (7%)
  local copies, waits for them, and re-layouts  1.89 us (2%)
    all_to_all x2, blocking collectives, exchange(): return lax.all_to_all(block, axes, 0, 0, tiled=True)  45.5 us
    ppermute x2, starting transfers between devices, shift_exchange(): lax.ppermute(high_edge, axis, forward)  9.15 us
    pallas_call x1, Pallas kernels, local(): call(functools.partial(output_kernel, count=count), out_shape=jax.ShapeDt...  5.98 us
    ppermute x2, waiting for transfers between devices, shift_exchange(): lax.ppermute(low_edge, axis, backward)  5.41 us
    ppermute x2, starting transfers between devices, shift_exchange(): lax.ppermute(low_edge, axis, backward)  4.67 us
    pallas_call x1, Pallas kernels, local(): call(hidden_kernel, out_shape=(jax.ShapeDtypeStruct((cx + 2, cy + 2, rows...  2.57 us
    unnamed x12, local copies, waits for them, and re-layouts  1.89 us
  transfers between devices with their start and end apart: 4, of which 2 were waited for; matrix products, arithmetic and copies ran while one was open for 0% of the time, Pallas kernels for 1%

profile of v3, /device:TPU:1, one launch (start us, length us, event | category | flops | bytes accessed | tf_op | source)
XLA Modules:
  0.0 76.2 jit_solution(18198423638122159187)
XLA Ops:
  0.0 0.0 copy-start.1
  0.0 0.0 copy-start.2
  0.0 0.9 %copy-done.2 = bf16[2,8,4096]{2,1,0:T(8,128)(2,1)S(1)} copy-done((bf16[2,8,4096]{2,1,0:T(8,128)(2,1)S(1)}, bf16[2,8,4096]{2,1,0:T(8,128)(2,1)}, u32[]{:S(2)}) %copy-start.2) | copy-done | bytes 131096
  0.9 0.1 rows.1.own_ref
  1.1 4.0 %collective-permute-start = (bf16[2,8,16,256]{3,2,1,0:T(8,128)(2,1)S(1)}, bf16[2,8,16,256]{3,2,1,0:T(8,128)(2,1)S(1)}, u32[]{:S(2)}, u32[]{:S(2)}) collective-permute-start(bf16[2,8,16,256]{3,2,1,0:T(8,128)(2,1)S(1)} %rows.1.own_ref), channel_id=1, source_target_pairs={{0,8},{8,16},{16,24},{24,32},{32,40},{40,48},{48,56},{56,64},{64,7... | collective-permute-start | bytes 393224 | tf_op jit(solution)/shard_map/ppermute | solution.py:29
  5.1 1.3 %collective-permute-start.1 = (bf16[2,8,16,256]{3,2,1,0:T(8,128)(2,1)S(1)}, bf16[2,8,16,256]{3,2,1,0:T(8,128)(2,1)S(1)}, u32[]{:S(2)}, u32[]{:S(2)}) collective-permute-start(bf16[2,8,16,256]{3,2,1,0:T(8,128)(2,1)S(1)} %rows.1.own_ref), channel_id=1, source_target_pairs={{8,0},{16,8},{24,16},{32,24},{40,32},{48,40},{56,48},{64,56},{72,6... | collective-permute-start | bytes 393224 | tf_op jit(solution)/shard_map/ppermute | solution.py:29
  6.4 0.0 copy-start
  6.4 0.9 %copy-done = bf16[1728,64]{0,1:T(8,128)(2,1)S(1)} copy-done((bf16[1728,64]{0,1:T(8,128)(2,1)S(1)}, bf16[1728,64]{0,1:T(8,128)(2,1)}, u32[]{:S(2)}) %copy-start) | copy-done | bytes 221208
  7.3 0.2 band.2.w_ref
  7.6 0.0 copy-done.1
  7.6 0.2 band.3.w_ref
  7.8 0.0 collective-permute-done.xlo_ref
  7.8 3.0 %collective-permute-done.1.xhi_ref = bf16[2,8,16,256]{3,2,1,0:T(8,128)(2,1)S(1)} collective-permute-done((bf16[2,8,16,256]{3,2,1,0:T(8,128)(2,1)S(1)}, bf16[2,8,16,256]{3,2,1,0:T(8,128)(2,1)S(1)}, u32[]{:S(2)}, u32[]{:S(2)}) %collective-permute-start.1) | collective-permute-done | bytes 131104 | tf_op jit(solution)/shard_map/ppermute | solution.py:29
  10.8 5.1 %collective-permute-start.2 = (bf16[6,2,16,256]{3,2,1,0:T(8,128)(2,1)S(1)}, bf16[6,2,16,256]{3,2,1,0:T(8,128)(2,1)S(1)}, u32[]{:S(2)}, u32[]{:S(2)}) collective-permute-start(bf16[6,2,16,256]{3,2,1,0:T(8,128)(2,1)S(1)} %get-tuple-element.16), channel_id=1, source_target_pairs={{0,1},{1,2},{2,3},{3,4},{4,5},{5,6},{6,7},{8,9},{9,10},{10,11},{11... | collective-permute-start | bytes 294920 | tf_op jit(solution)/shard_map/ppermute | solution.py:29
  16.0 3.4 %collective-permute-start.3 = (bf16[6,2,16,256]{3,2,1,0:T(8,128)(2,1)S(1)}, bf16[6,2,16,256]{3,2,1,0:T(8,128)(2,1)S(1)}, u32[]{:S(2)}, u32[]{:S(2)}) collective-permute-start(bf16[6,2,16,256]{3,2,1,0:T(8,128)(2,1)S(1)} %get-tuple-element.15), channel_id=1, source_target_pairs={{1,0},{2,1},{3,2},{4,3},{5,4},{6,5},{7,6},{9,8},{10,9},{11,10},{12... | collective-permute-start | bytes 294920 | tf_op jit(solution)/shard_map/ppermute | solution.py:29
  19.3 0.1 add_convert_fusion.inside_ref
  19.4 0.0 copy-start.3
  19.4 0.0 copy-start.4
  19.4 0.0 copy-start.5
  19.4 0.0 collective-permute-done.2.ylo_ref
  19.4 2.5 %collective-permute-done.3.yhi_ref = bf16[6,2,16,256]{3,2,1,0:T(8,128)(2,1)S(1)} collective-permute-done((bf16[6,2,16,256]{3,2,1,0:T(8,128)(2,1)S(1)}, bf16[6,2,16,256]{3,2,1,0:T(8,128)(2,1)S(1)}, u32[]{:S(2)}, u32[]{:S(2)}) %collective-permute-start.3) | collective-permute-done | bytes 98336 | tf_op jit(solution)/shard_map/ppermute | solution.py:29
  21.9 2.6 %hidden.1 = (f32[4,10,16,256]{3,2,1,0:T(8,128)S(1)}, f32[16,17,1,128]{3,2,1,0:T(1,128)S(1)}) custom-call(bf16[2,8,16,256]{3,2,1,0:T(8,128)(2,1)S(1)} %rows.1.own_ref, bf16[2,8,16,256]{3,2,1,0:T(8,128)(2,1)S(1)} %collective-permute-done.xlo_ref, bf16[2,8,16,256]{3,2,1,0:T(8,128)(2,1)S(1)} %collective-permute-done.1.xhi_ref, ...), custom_call_target="tpu_custom_call" | custom-call | tf_op jit(solution)/shard_map/hidden/pallas_call | solution.py:240
  24.5 29.2 %all_to_all.10.in_ref = f32[16,17,1,128]{3,2,1,0:T(1,128)S(1)} all-to-all(f32[16,17,1,128]{3,2,1,0:T(1,128)S(1)} %get-tuple-element.12), channel_id=1, replica_groups=mesh['gx_0'=16,'gx_1'=4,'gy_0'=4,'gy_1'=2] {'gx_0'}, dimensions={0} | all-to-all | bytes 278528 | tf_op jit(solution)/shard_map/all_to_all | solution.py:215
  53.7 0.2 relay.1
  53.9 16.3 %all_to_all.11.pay_ref = f32[32,17,1,128]{3,2,1,0:T(1,128)S(1)} all-to-all(f32[32,17,1,128]{3,2,1,0:T(1,128)S(1)} %relay.1), channel_id=1, replica_groups=mesh['gx_0'=16,'gx_1'=4,'gy_0'=4,'gy_1'=2] {'gx_1','gy_0','gy_1'}, dimensions={0} | all-to-all | bytes 557056 | tf_op jit(solution)/shard_map/all_to_all | solution.py:215
  70.2 0.0 copy-done.3
  70.2 0.0 copy-done.4
  70.2 0.0 copy-done.5
  70.2 6.0 %output.1 = bf16[2,8,4096]{2,1,0:T(8,128)(2,1)} custom-call(s32[4]{0:T(128)S(1)} %add_convert_fusion.inside_ref, f32[32,17,1,128]{3,2,1,0:T(1,128)S(1)} %all_to_all.11.pay_ref, f32[4,10,16,256]{3,2,1,0:T(8,128)S(1)} %get-tuple-element.13.hidden_ref, f32[1,64]{1,0:T(1,128)S(1)} %bitcast.11, f32[1,64]{1,0:T(1,128)S(1)} %bitcast.12, ...), custom_call_target="tpu_custom_call" | custom-call | tf_op jit(solution)/shard_map/output/pallas_call | solution.py:262
  (1 shorter events, 0.0 us)
Async XLA Ops:
  0.0 7.6 %copy-start.1 = (bf16[1728,64]{0,1:T(8,128)(2,1)S(1)}, bf16[1728,64]{0,1:T(8,128)(2,1)}, u32[]{:S(2)}) copy-start(bf16[1728,64]{0,1:T(8,128)(2,1)} %param.10) | copy-start | bytes 663556
  0.0 0.9 %copy-start.2 = (bf16[2,8,4096]{2,1,0:T(8,128)(2,1)S(1)}, bf16[2,8,4096]{2,1,0:T(8,128)(2,1)}, u32[]{:S(2)}) copy-start(bf16[2,8,4096]{2,1,0:T(8,128)(2,1)} %v_ref.1) | copy-start | bytes 393220
  1.1 6.8 %collective-permute-start = (bf16[2,8,16,256]{3,2,1,0:T(8,128)(2,1)S(1)}, bf16[2,8,16,256]{3,2,1,0:T(8,128)(2,1)S(1)}, u32[]{:S(2)}, u32[]{:S(2)}) collective-permute-start(bf16[2,8,16,256]{3,2,1,0:T(8,128)(2,1)S(1)} %rows.1.own_ref), channel_id=1, source_target_pairs={{0,8},{8,16},{16,24},{24,32},{32,40},{40,48},{48,56},{56,64},{64,7... | collective-permute-start | bytes 393224 | tf_op jit(solution)/shard_map/ppermute | solution.py:29
  5.1 5.7 %collective-permute-start.1 = (bf16[2,8,16,256]{3,2,1,0:T(8,128)(2,1)S(1)}, bf16[2,8,16,256]{3,2,1,0:T(8,128)(2,1)S(1)}, u32[]{:S(2)}, u32[]{:S(2)}) collective-permute-start(bf16[2,8,16,256]{3,2,1,0:T(8,128)(2,1)S(1)} %rows.1.own_ref), channel_id=1, source_target_pairs={{8,0},{16,8},{24,16},{32,24},{40,32},{48,40},{56,48},{64,56},{72,6... | collective-permute-start | bytes 393224 | tf_op jit(solution)/shard_map/ppermute | solution.py:29
  6.4 0.9 %copy-start = (bf16[1728,64]{0,1:T(8,128)(2,1)S(1)}, bf16[1728,64]{0,1:T(8,128)(2,1)}, u32[]{:S(2)}) copy-start(bf16[1728,64]{0,1:T(8,128)(2,1)} %param.7) | copy-start | bytes 663556
  10.8 8.6 %collective-permute-start.2 = (bf16[6,2,16,256]{3,2,1,0:T(8,128)(2,1)S(1)}, bf16[6,2,16,256]{3,2,1,0:T(8,128)(2,1)S(1)}, u32[]{:S(2)}, u32[]{:S(2)}) collective-permute-start(bf16[6,2,16,256]{3,2,1,0:T(8,128)(2,1)S(1)} %get-tuple-element.16), channel_id=1, source_target_pairs={{0,1},{1,2},{2,3},{3,4},{4,5},{5,6},{6,7},{8,9},{9,10},{10,11},{11... | collective-permute-start | bytes 294920 | tf_op jit(solution)/shard_map/ppermute | solution.py:29
  16.0 5.9 %collective-permute-start.3 = (bf16[6,2,16,256]{3,2,1,0:T(8,128)(2,1)S(1)}, bf16[6,2,16,256]{3,2,1,0:T(8,128)(2,1)S(1)}, u32[]{:S(2)}, u32[]{:S(2)}) collective-permute-start(bf16[6,2,16,256]{3,2,1,0:T(8,128)(2,1)S(1)} %get-tuple-element.15), channel_id=1, source_target_pairs={{1,0},{2,1},{3,2},{4,3},{5,4},{6,5},{7,6},{9,8},{10,9},{11,10},{12... | collective-permute-start | bytes 294920 | tf_op jit(solution)/shard_map/ppermute | solution.py:29
  19.4 50.8 %copy-start.3 = (f32[64]{0:T(128)S(1)}, f32[64]{0:T(128)}, u32[]{:S(2)}) copy-start(f32[64]{0:T(128)} %param.8) | copy-start | bytes 772
  19.4 50.8 %copy-start.4 = (f32[64]{0:T(128)S(1)}, f32[64]{0:T(128)}, u32[]{:S(2)}) copy-start(f32[64]{0:T(128)} %param.9) | copy-start | bytes 772
  19.4 50.8 %copy-start.5 = (f32[64]{0:T(128)S(1)}, f32[64]{0:T(128)}, u32[]{:S(2)}) copy-start(f32[64]{0:T(128)} %param.11) | copy-start | bytes 772

commit v4 on v2

--- a/solution.py
+++ b/solution.py
@@ -22,14 +22,16 @@
     return pltpu.CompilerParams(vmem_limit_bytes=48 * 1024 * 1024)
 
 
-def shift_exchange(low_edge, high_edge, axis):
-    count = lax.axis_size(axis)
-    forward = [(i, i + 1) for i in range(count - 1)]
-    backward = [(target, source) for source, target in forward]
-    return lax.ppermute(high_edge, axis, forward), lax.ppermute(low_edge, axis, backward)
-
-
-def rows_kernel(v_ref, o_ref, f_ref):
+def group_size(axes):
+    return functools.reduce(lambda total, axis: total * lax.axis_size(axis), axes, 1)
+
+
+def swap(block, axis, first):
+    pairs = [(i, i + 1) for i in range(first, lax.axis_size(axis) - 1, 2)]
+    return lax.ppermute(block, axis, pairs + [(target, source) for source, target in pairs])
+
+
+def to_rows(v_ref, o_ref, f_ref):
     slabs, sub, merged = v_ref.shape
     rows, lanes = o_ref.shape[2:]
     for x in range(slabs):
@@ -41,6 +43,21 @@
                 ].astype(F32)
     for h in range(lanes // 128):
         o_ref[:, :, :, h * 128 : (h + 1) * 128] = f_ref[h].astype(BF16).reshape(slabs, sub, rows, 128)
+
+
+def rows_kernel(v_ref, o_ref, f_ref):
+    to_rows(v_ref, o_ref, f_ref)
+
+
+def edges_kernel(own_ref, xa_ref, xb_ref, xs_ref, ea_ref, eb_ref, fa_ref, fb_ref):
+    cx, cy = own_ref.shape[:2]
+    odd_x, odd_y = lax.axis_index(GX) & 1, lax.axis_index(GY) & 1
+    to_rows(xa_ref, xs_ref.at[1 - odd_x], fa_ref)
+    to_rows(xb_ref, xs_ref.at[odd_x], fb_ref)
+    for edge_ref, first in ((ea_ref, (1 - odd_y) * (cy - 2)), (eb_ref, odd_y * (cy - 2))):
+        edge_ref[0:2] = xs_ref[0, :, pl.ds(first, 2)]
+        edge_ref[2 : 2 + cx] = own_ref[:, pl.ds(first, 2)]
+        edge_ref[2 + cx : 4 + cx] = xs_ref[1, :, pl.ds(first, 2)]
 
 
 def band_kernel(w_ref, o_ref):
@@ -92,15 +109,16 @@
     return lax.broadcasted_iota(jnp.int32, (n, n), 0), lax.broadcasted_iota(jnp.int32, (n, n), 1)
 
 
-def hidden_kernel(own_ref, xlo_ref, xhi_ref, ylo_ref, yhi_ref, w_ref, hidden_ref, pay_ref, f_ref, x_ref):
+def hidden_kernel(own_ref, xs_ref, ya_ref, yb_ref, w_ref, hidden_ref, pay_ref, f_ref, x_ref):
     rows = own_ref.shape[2]
     cx, cy = own_ref.shape[:2]
     clear_ends(f_ref, rows)
-    f_ref[:, 0:2, 8 : 8 + rows, :] = ylo_ref[...].astype(F32)
-    f_ref[0:2, 2 : 2 + cy, 8 : 8 + rows, :] = xlo_ref[...].astype(F32)
+    f_ref[0:2, 2 : 2 + cy, 8 : 8 + rows, :] = xs_ref[0].astype(F32)
     f_ref[2 : 2 + cx, 2 : 2 + cy, 8 : 8 + rows, :] = own_ref[...].astype(F32)
-    f_ref[2 + cx : 4 + cx, 2 : 2 + cy, 8 : 8 + rows, :] = xhi_ref[...].astype(F32)
-    f_ref[:, 2 + cy : 4 + cy, 8 : 8 + rows, :] = yhi_ref[...].astype(F32)
+    f_ref[2 + cx : 4 + cx, 2 : 2 + cy, 8 : 8 + rows, :] = xs_ref[1].astype(F32)
+    odd_y = lax.axis_index(GY) & 1
+    f_ref[:, pl.ds((1 - odd_y) * (cy + 2), 2), 8 : 8 + rows, :] = ya_ref[...].astype(F32)
+    f_ref[:, pl.ds(odd_y * (cy + 2), 2), 8 : 8 + rows, :] = yb_ref[...].astype(F32)
     widen(f_ref, x_ref)
     hidden_ref[...] = banded_conv(x_ref, w_ref).reshape(hidden_ref.shape)
     own = hidden_ref[1 : 1 + cx, 1 : 1 + cy].reshape(cx * cy * rows, 256)
@@ -173,7 +191,7 @@
 
 
 def output_kernel(
-    inside_ref, pay_ref, hidden_ref, gain_ref, shift_ref, w_ref, bias_ref, out_ref, p_ref, f_ref, x_ref, o_ref, *, count
+    pay_ref, hidden_ref, gain_ref, shift_ref, w_ref, bias_ref, out_ref, p_ref, f_ref, x_ref, o_ref, *, count
 ):
     nx, ny, rows, lanes = hidden_ref.shape
     mean, sigma, eye = moments(pay_ref, p_ref, count)
@@ -190,9 +208,15 @@
     act = jnp.maximum(gain * normalized + shift, 0.0).reshape(hidden_ref.shape)
     clear_ends(f_ref, rows)
     f_ref[:, :, 8 : 8 + rows, :] = act
-    for flag, edge in ((0, f_ref.at[0]), (1, f_ref.at[nx - 1]), (2, f_ref.at[:, 0]), (3, f_ref.at[:, ny - 1])):
-
-        @pl.when(inside_ref[flag] == 0)
+    at_x, at_y = lax.axis_index(GX), lax.axis_index(GY)
+    for outside, edge in (
+        (at_x == 0, f_ref.at[0]),
+        (at_x == group_size(GX) - 1, f_ref.at[nx - 1]),
+        (at_y == 0, f_ref.at[:, 0]),
+        (at_y == group_size(GY) - 1, f_ref.at[:, ny - 1]),
+    ):
+
+        @pl.when(outside)
         def _(edge=edge):
             edge[...] = jnp.zeros_like(edge)
 
@@ -215,10 +239,6 @@
     return lax.all_to_all(block, axes, 0, 0, tiled=True)
 
 
-def group_size(axes):
-    return functools.reduce(lambda total, axis: total * lax.axis_size(axis), axes, 1)
-
-
 def local(volume, conv_first, gain, shift, conv_second, bias_second):
     width = bias_second.shape[0]
     cx, cy, merged = volume.shape
@@ -226,17 +246,20 @@
     rows = merged // lanes
     count = float(cx * group_size(GX) * cy * group_size(GY) * (merged // width))
     call = functools.partial(pl.pallas_call, compiler_params=params())
-    own = call(
-        rows_kernel,
-        out_shape=jax.ShapeDtypeStruct((cx, cy, rows, lanes), BF16),
-        scratch_shapes=[pltpu.VMEM((lanes // 128, cx * cy * rows, 128), F32)],
-        name="rows",
-    )(volume)
+    xa, xb = swap(volume, GX, 0), swap(volume, GX, 1)
+    block = jax.ShapeDtypeStruct((cx, cy, rows, lanes), BF16)
+    half = pltpu.VMEM((lanes // 128, cx * cy * rows, 128), F32)
+    own = call(rows_kernel, out_shape=block, scratch_shapes=[half], name="rows")(volume)
     band = call(band_kernel, out_shape=jax.ShapeDtypeStruct((lanes, 54 * width), BF16), name="band")
     first, second = band(conv_first.T), band(conv_second.T)
-    xlo, xhi = shift_exchange(own[:2], own[cx - 2 :], GX)
-    sides = jnp.concatenate([xlo, own, xhi], axis=0)
-    ylo, yhi = shift_exchange(sides[:, :2], sides[:, cy - 2 :], GY)
+    edge = jax.ShapeDtypeStruct((cx + 4, 2, rows, lanes), BF16)
+    xs, ea, eb = call(
+        edges_kernel,
+        out_shape=(jax.ShapeDtypeStruct((2,) + block.shape, BF16), edge, edge),
+        scratch_shapes=[half, half],
+        name="edges",
+    )(own, xa, xb)
+    ya, yb = swap(ea, GY, 0), swap(eb, GY, 1)
     hidden, pay = call(
         hidden_kernel,
         out_shape=(
@@ -248,21 +271,17 @@
             pltpu.VMEM((cx + 4, cy + 4, rows, 6 * width), BF16),
         ],
         name="hidden",
-    )(own, xlo, xhi, ylo, yhi, first)
+    )(own, xs, ya, yb, first)
     rest = GX[1:] + GY
+    pay, second = lax.optimization_barrier((pay, second))
     pay = exchange(pay, GX[:1])
     pay = call(
         relay_kernel, out_shape=jax.ShapeDtypeStruct((group_size(rest), PAY, 1, 128), F32), name="relay"
     )(pay)
     pay = exchange(pay, rest)
-    at_x, at_y = lax.axis_index(GX), lax.axis_index(GY)
-    inside = jnp.stack([at_x > 0, at_x < group_size(GX) - 1, at_y > 0, at_y < group_size(GY) - 1]).astype(jnp.int32)
-    in_vmem = pl.BlockSpec(memory_space=pltpu.VMEM)
     return call(
         functools.partial(output_kernel, count=count),
         out_shape=jax.ShapeDtypeStruct((cx, cy, merged), BF16),
-        in_specs=[pl.BlockSpec(memory_space=pltpu.SMEM)] + [in_vmem] * 6,
-        out_specs=in_vmem,
         scratch_shapes=[
             pltpu.VMEM((24, 128), F32),
             pltpu.VMEM((cx + 2, cy + 2, rows + 16, lanes), F32),
@@ -270,7 +289,7 @@
             pltpu.VMEM((lanes // 128, cx * cy * rows, 128), F32),
         ],
         name="output",
-    )(inside, pay, hidden, gain[None], shift[None], second, bias_second[None])
+    )(pay, hidden, gain[None], shift[None], second, bias_second[None])
 
 
 def solution(mesh):

time: 77.5 us -> 72.7 us (0.938)
  blocking collectives: 29.3 us -> 41.3 us
  waiting for transfers between devices: 14.5 us -> 4.1 us
  starting transfers between devices: 21.3 us -> 16 us
  Pallas kernels: 10 us -> 9.02 us
    all_to_all x1 -> x2, blocking collectives: 29.3 us -> 41.3 us  [exchange(): return lax.all_to_all(block, axes, 0, 0, tiled=True)]
    all_to_all x1 -> x0, waiting for transfers between devices: 8.72 us -> none  [exchange(): return lax.all_to_all(block, axes, 0, 0, tiled=True)]
    all_to_all x1 -> x0, starting transfers between devices: 7.45 us -> none  [exchange(): return lax.all_to_all(block, axes, 0, 0, tiled=True)]
    ppermute x4, starting transfers between devices: 13.8 us -> 16 us  [swap(): lax.ppermute(block, axis, pairs + [(target, source) for source, target in...]
    ppermute x4, waiting for transfers between devices: 5.76 us -> 4.1 us  [swap(): lax.ppermute(block, axis, pairs + [(target, source) for source, target in...]
  transfers between devices with their start and end apart: 5 -> 4, of which waited for: 4 -> 2; matrix products, arithmetic and copies ran while one was open for 0% -> 0% of each run, Pallas kernels for 1% -> 1%
where the time goes in v4:
time: 72.7 us; the launch traced here: 72.4 us
  blocking collectives  41.3 us (57%)
  starting transfers between devices  16 us (22%)
  Pallas kernels  9.02 us (12%)
  waiting for transfers between devices  4.1 us (6%)
  local copies, waits for them, and re-layouts  1.86 us (3%)
    all_to_all x2, blocking collectives, exchange(): return lax.all_to_all(block, axes, 0, 0, tiled=True)  41.3 us
    ppermute x4, starting transfers between devices, swap(): lax.ppermute(block, axis, pairs + [(target, source) for source, target in...  16 us
    pallas_call x1, Pallas kernels, local(): call(functools.partial(output_kernel, count=count), out_shape=jax.ShapeDt...  5.43 us
    ppermute x4, waiting for transfers between devices, swap(): lax.ppermute(block, axis, pairs + [(target, source) for source, target in...  4.1 us
    pallas_call x1, Pallas kernels, local(): call(hidden_kernel, out_shape=(jax.ShapeDtypeStruct((cx + 2, cy + 2, rows...  2.64 us
    unnamed x12, local copies, waits for them, and re-layouts  1.86 us
  transfers between devices with their start and end apart: 4, of which 2 were waited for; matrix products, arithmetic and copies ran while one was open for 0% of the time, Pallas kernels for 1%

profile of v4, /device:TPU:1, one launch (start us, length us, event | category | flops | bytes accessed | tf_op | source)
XLA Modules:
  0.0 72.4 jit_solution(15404116615029816816)
XLA Ops:
  0.0 0.0 copy-start.1
  0.0 0.8 %collective-permute-start.1 = (bf16[2,8,4096]{2,1,0:T(8,128)(2,1)}, bf16[2,8,4096]{2,1,0:T(8,128)(2,1)S(1)}, u32[]{:S(2)}, u32[]{:S(2)}) collective-permute-start(bf16[2,8,4096]{2,1,0:T(8,128)(2,1)} %v_ref.1), channel_id=1, source_target_pairs={{8,16},{24,32},{40,48},{56,64},{72,80},{88,96},{104,112},{120,128}... | collective-permute-start | bytes 393224 | tf_op jit(solution)/shard_map/ppermute | solution.py:31
  0.8 6.6 %collective-permute-start = (bf16[2,8,4096]{2,1,0:T(8,128)(2,1)}, bf16[2,8,4096]{2,1,0:T(8,128)(2,1)S(1)}, u32[]{:S(2)}, u32[]{:S(2)}) collective-permute-start(bf16[2,8,4096]{2,1,0:T(8,128)(2,1)} %v_ref.1), channel_id=1, source_target_pairs={{0,8},{16,24},{32,40},{48,56},{64,72},{80,88},{96,104},{112,120},{... | collective-permute-start | bytes 393224 | tf_op jit(solution)/shard_map/ppermute | solution.py:31
  7.4 0.0 copy-start.2
  7.4 0.9 %copy-done.2 = bf16[2,8,4096]{2,1,0:T(8,128)(2,1)S(1)} copy-done((bf16[2,8,4096]{2,1,0:T(8,128)(2,1)S(1)}, bf16[2,8,4096]{2,1,0:T(8,128)(2,1)}, u32[]{:S(2)}) %copy-start.2) | copy-done | bytes 131096
  8.3 0.1 rows.1.own_ref
  8.4 0.0 collective-permute-done.1.xb_ref
  8.4 1.5 %collective-permute-done.xa_ref = bf16[2,8,4096]{2,1,0:T(8,128)(2,1)S(1)} collective-permute-done((bf16[2,8,4096]{2,1,0:T(8,128)(2,1)}, bf16[2,8,4096]{2,1,0:T(8,128)(2,1)S(1)}, u32[]{:S(2)}, u32[]{:S(2)}) %collective-permute-start) | collective-permute-done | bytes 131104 | tf_op jit(solution)/shard_map/ppermute | solution.py:31
  9.9 0.2 edges.1
  10.2 6.7 %collective-permute-start.2 = (bf16[6,2,16,256]{3,2,1,0:T(8,128)(2,1)S(1)}, bf16[6,2,16,256]{3,2,1,0:T(8,128)(2,1)S(1)}, u32[]{:S(2)}, u32[]{:S(2)}) collective-permute-start(bf16[6,2,16,256]{3,2,1,0:T(8,128)(2,1)S(1)} %get-tuple-element.13), channel_id=1, source_target_pairs={{0,1},{2,3},{4,5},{6,7},{1,0},{3,2},{5,4},{7,6},{8,9},{10,11},{12,... | collective-permute-start | bytes 294920 | tf_op jit(solution)/shard_map/ppermute | solution.py:31
  16.9 1.9 %collective-permute-start.3 = (bf16[6,2,16,256]{3,2,1,0:T(8,128)(2,1)S(1)}, bf16[6,2,16,256]{3,2,1,0:T(8,128)(2,1)S(1)}, u32[]{:S(2)}, u32[]{:S(2)}) collective-permute-start(bf16[6,2,16,256]{3,2,1,0:T(8,128)(2,1)S(1)} %get-tuple-element.14), channel_id=1, source_target_pairs={{1,2},{3,4},{5,6},{2,1},{4,3},{6,5},{9,10},{11,12},{13,14},{10,9},... | collective-permute-start | bytes 294920 | tf_op jit(solution)/shard_map/ppermute | solution.py:31
  18.8 0.0 copy-start
  18.8 0.9 %copy-done = bf16[1728,64]{0,1:T(8,128)(2,1)S(1)} copy-done((bf16[1728,64]{0,1:T(8,128)(2,1)S(1)}, bf16[1728,64]{0,1:T(8,128)(2,1)}, u32[]{:S(2)}) %copy-start) | copy-done | bytes 221208
  19.8 0.2 band.2.w_ref
  20.0 0.0 copy-done.1
  20.0 0.2 band.3.w_ref
  20.2 0.0 collective-permute-done.2.ya_ref
  20.2 2.6 %collective-permute-done.3.yb_ref = bf16[6,2,16,256]{3,2,1,0:T(8,128)(2,1)S(1)} collective-permute-done((bf16[6,2,16,256]{3,2,1,0:T(8,128)(2,1)S(1)}, bf16[6,2,16,256]{3,2,1,0:T(8,128)(2,1)S(1)}, u32[]{:S(2)}, u32[]{:S(2)}) %collective-permute-start.3) | collective-permute-done | bytes 98336 | tf_op jit(solution)/shard_map/ppermute | solution.py:31
  22.8 0.0 copy-start.3
  22.8 0.0 copy-start.4
  22.8 0.0 copy-start.5
  22.8 2.6 %hidden.1 = (f32[4,10,16,256]{3,2,1,0:T(8,128)S(1)}, f32[16,17,1,128]{3,2,1,0:T(1,128)S(1)}) custom-call(bf16[2,8,16,256]{3,2,1,0:T(8,128)(2,1)S(1)} %rows.1.own_ref, bf16[2,2,8,16,256]{4,3,2,1,0:T(8,128)(2,1)S(1)} %get-tuple-element.12.xs_ref, bf16[6,2,16,256]{3,2,1,0:T(8,128)(2,1)S(1)} %collective-permute-done.2.ya_ref, ...), custom_call_target="tpu_custom_call" | custom-call | tf_op jit(solution)/shard_map/hidden/pallas_call | solution.py:263
  25.5 26.4 %all_to_all.10.in_ref = f32[16,17,1,128]{3,2,1,0:T(1,128)S(1)} all-to-all(f32[16,17,1,128]{3,2,1,0:T(1,128)S(1)} %get-tuple-element.16), channel_id=1, replica_groups=mesh['gx_0'=16,'gx_1'=4,'gy_0'=4,'gy_1'=2] {'gx_0'}, dimensions={0} | all-to-all | bytes 278528 | tf_op jit(solution)/shard_map/all_to_all | solution.py:239
  51.8 0.2 relay.1
  52.0 15.0 %all_to_all.11.pay_ref = f32[32,17,1,128]{3,2,1,0:T(1,128)S(1)} all-to-all(f32[32,17,1,128]{3,2,1,0:T(1,128)S(1)} %relay.1), channel_id=1, replica_groups=mesh['gx_0'=16,'gx_1'=4,'gy_0'=4,'gy_1'=2] {'gx_1','gy_0','gy_1'}, dimensions={0} | all-to-all | bytes 557056 | tf_op jit(solution)/shard_map/all_to_all | solution.py:239
  67.0 0.0 copy-done.3
  67.0 0.0 copy-done.4
  67.0 0.0 copy-done.5
  67.0 5.4 %output.1 = bf16[2,8,4096]{2,1,0:T(8,128)(2,1)} custom-call(f32[32,17,1,128]{3,2,1,0:T(1,128)S(1)} %all_to_all.11.pay_ref, f32[4,10,16,256]{3,2,1,0:T(8,128)S(1)} %get-tuple-element.17.hidden_ref, f32[1,64]{1,0:T(1,128)S(1)} %bitcast.7, f32[1,64]{1,0:T(1,128)S(1)} %bitcast.8, bf16[256,3456]{1,0:T(8,128)(2,1)S(1)} %band.3.w_ref, f32[1,64]{1,0:T(1,128)S(1)} %bitcast.9), custom_call_target="tpu_custom_call" | custom-call | tf_op jit(solution)/shard_map/output/pallas_call | solution.py:282
Async XLA Ops:
  0.0 20.0 %copy-start.1 = (bf16[1728,64]{0,1:T(8,128)(2,1)S(1)}, bf16[1728,64]{0,1:T(8,128)(2,1)}, u32[]{:S(2)}) copy-start(bf16[1728,64]{0,1:T(8,128)(2,1)} %param.10) | copy-start | bytes 663556
  0.0 8.4 %collective-permute-start.1 = (bf16[2,8,4096]{2,1,0:T(8,128)(2,1)}, bf16[2,8,4096]{2,1,0:T(8,128)(2,1)S(1)}, u32[]{:S(2)}, u32[]{:S(2)}) collective-permute-start(bf16[2,8,4096]{2,1,0:T(8,128)(2,1)} %v_ref.1), channel_id=1, source_target_pairs={{8,16},{24,32},{40,48},{56,64},{72,80},{88,96},{104,112},{120,128}... | collective-permute-start | bytes 393224 | tf_op jit(solution)/shard_map/ppermute | solution.py:31
  0.8 9.1 %collective-permute-start = (bf16[2,8,4096]{2,1,0:T(8,128)(2,1)}, bf16[2,8,4096]{2,1,0:T(8,128)(2,1)S(1)}, u32[]{:S(2)}, u32[]{:S(2)}) collective-permute-start(bf16[2,8,4096]{2,1,0:T(8,128)(2,1)} %v_ref.1), channel_id=1, source_target_pairs={{0,8},{16,24},{32,40},{48,56},{64,72},{80,88},{96,104},{112,120},{... | collective-permute-start | bytes 393224 | tf_op jit(solution)/shard_map/ppermute | solution.py:31
  7.4 0.9 %copy-start.2 = (bf16[2,8,4096]{2,1,0:T(8,128)(2,1)S(1)}, bf16[2,8,4096]{2,1,0:T(8,128)(2,1)}, u32[]{:S(2)}) copy-start(bf16[2,8,4096]{2,1,0:T(8,128)(2,1)} %v_ref.1) | copy-start | bytes 393220
  10.2 10.1 %collective-permute-start.2 = (bf16[6,2,16,256]{3,2,1,0:T(8,128)(2,1)S(1)}, bf16[6,2,16,256]{3,2,1,0:T(8,128)(2,1)S(1)}, u32[]{:S(2)}, u32[]{:S(2)}) collective-permute-start(bf16[6,2,16,256]{3,2,1,0:T(8,128)(2,1)S(1)} %get-tuple-element.13), channel_id=1, source_target_pairs={{0,1},{2,3},{4,5},{6,7},{1,0},{3,2},{5,4},{7,6},{8,9},{10,11},{12,... | collective-permute-start | bytes 294920 | tf_op jit(solution)/shard_map/ppermute | solution.py:31
  16.9 5.9 %collective-permute-start.3 = (bf16[6,2,16,256]{3,2,1,0:T(8,128)(2,1)S(1)}, bf16[6,2,16,256]{3,2,1,0:T(8,128)(2,1)S(1)}, u32[]{:S(2)}, u32[]{:S(2)}) collective-permute-start(bf16[6,2,16,256]{3,2,1,0:T(8,128)(2,1)S(1)} %get-tuple-element.14), channel_id=1, source_target_pairs={{1,2},{3,4},{5,6},{2,1},{4,3},{6,5},{9,10},{11,12},{13,14},{10,9},... | collective-permute-start | bytes 294920 | tf_op jit(solution)/shard_map/ppermute | solution.py:31
  18.8 0.9 %copy-start = (bf16[1728,64]{0,1:T(8,128)(2,1)S(1)}, bf16[1728,64]{0,1:T(8,128)(2,1)}, u32[]{:S(2)}) copy-start(bf16[1728,64]{0,1:T(8,128)(2,1)} %param.7) | copy-start | bytes 663556
  22.8 44.2 %copy-start.3 = (f32[64]{0:T(128)S(1)}, f32[64]{0:T(128)}, u32[]{:S(2)}) copy-start(f32[64]{0:T(128)} %param.8) | copy-start | bytes 772
  22.8 44.2 %copy-start.4 = (f32[64]{0:T(128)S(1)}, f32[64]{0:T(128)}, u32[]{:S(2)}) copy-start(f32[64]{0:T(128)} %param.9) | copy-start | bytes 772
  22.8 44.2 %copy-start.5 = (f32[64]{0:T(128)S(1)}, f32[64]{0:T(128)}, u32[]{:S(2)}) copy-start(f32[64]{0:T(128)} %param.11) | copy-start | bytes 772

commit v5 on v4

--- a/solution.py
+++ b/solution.py
@@ -109,7 +109,30 @@
     return lax.broadcasted_iota(jnp.int32, (n, n), 0), lax.broadcasted_iota(jnp.int32, (n, n), 1)
 
 
-def hidden_kernel(own_ref, xs_ref, ya_ref, yb_ref, w_ref, hidden_ref, pay_ref, f_ref, x_ref):
+def transposed(a):
+    return jnp.transpose(a)
+
+
+def split(a):
+    high = a.astype(BF16)
+    return high, (a - high.astype(F32)).astype(BF16)
+
+
+def dot3(a, b):
+    dot = functools.partial(jnp.dot, preferred_element_type=F32)
+    a0, a1 = split(a)
+    b0, b1 = split(b)
+    return dot(a0, b0) + (dot(a0, b1) + dot(a1, b0))
+
+
+def fold_blocks(wide):
+    total = wide[0:64, 0:64]
+    for k in range(1, PACK):
+        total = total + wide[k * 64 : (k + 1) * 64, k * 64 : (k + 1) * 64]
+    return total
+
+
+def hidden_kernel(own_ref, xs_ref, yb_ref, ya_ref, w_ref, hidden_ref, pay_ref, f_ref, x_ref):
     rows = own_ref.shape[2]
     cx, cy = own_ref.shape[:2]
     clear_ends(f_ref, rows)
@@ -122,13 +145,19 @@
     widen(f_ref, x_ref)
     hidden_ref[...] = banded_conv(x_ref, w_ref).reshape(hidden_ref.shape)
     own = hidden_ref[1 : 1 + cx, 1 : 1 + cy].reshape(cx * cy * rows, 256)
-    wide = lax.dot_general(own, own, (((0,), (0,)), ((), ())), precision=HIGHEST, preferred_element_type=F32)
     sums = jnp.sum(own, axis=0, keepdims=True)
-    gram = wide[0:64, 0:64]
     total = sums[:, 0:64]
     for k in range(1, PACK):
-        gram = gram + wide[k * 64 : (k + 1) * 64, k * 64 : (k + 1) * 64]
         total = total + sums[:, k * 64 : (k + 1) * 64]
+    cells = float(cx * cy * rows * PACK)
+    high, low = split(own - jnp.concatenate([total / cells] * PACK, axis=1))
+    outer = functools.partial(
+        lax.dot_general, dimension_numbers=(((0,), (0,)), ((), ())), preferred_element_type=F32
+    )
+    mixed = fold_blocks(outer(high, low))
+    i, j = square_iota(64)
+    column = jnp.sum(jnp.where(i == j, total, 0.0), axis=1, keepdims=True)
+    gram = fold_blocks(outer(high, high)) + (mixed + transposed(mixed)) + column * (total / cells)
     i, j = square_iota(32)
     low = gram[32:, 32:]
     tri = jnp.where(j >= i, gram[:32, :32], low)
@@ -146,10 +175,6 @@
     total = jnp.sum(in_ref[...], axis=0)
     for p in range(out_ref.shape[0]):
         out_ref[p] = total
-
-
-def transposed(a):
-    return jnp.transpose(a)
 
 
 def moments(pay_ref, p_ref, count):
@@ -180,13 +205,12 @@
 
 
 def newton_whiten(sigma, eye):
-    dot = functools.partial(jnp.dot, precision=HIGHEST, preferred_element_type=F32)
     trace = jnp.sum(jnp.sum(sigma * eye, axis=1, keepdims=True), axis=0, keepdims=True)
     normed = sigma / trace
     proj = 1.5 * eye - 0.5 * normed
     for _ in range(NEWTON - 1):
-        both = dot(proj, jnp.concatenate([proj, normed], axis=1))
-        proj = 1.5 * proj - 0.5 * dot(both[:, 0:64], both[:, 64:128])
+        both = dot3(proj, jnp.concatenate([proj, normed], axis=1))
+        proj = 1.5 * proj - 0.5 * dot3(both[:, 0:64], both[:, 64:128])
     return proj / jnp.sqrt(trace)
 
 
@@ -204,7 +228,7 @@
     gain = jnp.concatenate([gain_ref[...]] * PACK, axis=1)
     shift = jnp.concatenate([shift_ref[...]] * PACK, axis=1)
     centered = hidden_ref[...].reshape(nx * ny * rows, lanes) - mean
-    normalized = jnp.dot(centered, wide, precision=HIGHEST, preferred_element_type=F32)
+    normalized = dot3(centered, wide)
     act = jnp.maximum(gain * normalized + shift, 0.0).reshape(hidden_ref.shape)
     clear_ends(f_ref, rows)
     f_ref[:, :, 8 : 8 + rows, :] = act
@@ -252,6 +276,7 @@
     own = call(rows_kernel, out_shape=block, scratch_shapes=[half], name="rows")(volume)
     band = call(band_kernel, out_shape=jax.ShapeDtypeStruct((lanes, 54 * width), BF16), name="band")
     first, second = band(conv_first.T), band(conv_second.T)
+    xb, first, second = lax.optimization_barrier((xb, first, second))
     edge = jax.ShapeDtypeStruct((cx + 4, 2, rows, lanes), BF16)
     xs, ea, eb = call(
         edges_kernel,
@@ -259,26 +284,26 @@
         scratch_shapes=[half, half],
         name="edges",
     )(own, xa, xb)
-    ya, yb = swap(ea, GY, 0), swap(eb, GY, 1)
+    yb = swap(eb, GY, 1)
+    ya = swap(ea, GY, 0)
     hidden, pay = call(
         hidden_kernel,
         out_shape=(
             jax.ShapeDtypeStruct((cx + 2, cy + 2, rows, lanes), F32),
-            jax.ShapeDtypeStruct((group_size(GX[:1]), PAY, 1, 128), F32),
+            jax.ShapeDtypeStruct((group_size(GX[1:] + GY), PAY, 1, 128), F32),
         ),
         scratch_shapes=[
             pltpu.VMEM((cx + 4, cy + 4, rows + 16, lanes), F32),
             pltpu.VMEM((cx + 4, cy + 4, rows, 6 * width), BF16),
         ],
         name="hidden",
-    )(own, xs, ya, yb, first)
-    rest = GX[1:] + GY
-    pay, second = lax.optimization_barrier((pay, second))
-    pay = exchange(pay, GX[:1])
+    )(own, xs, yb, ya, first)
+    rest, line = GX[1:] + GY, GX[:1]
+    pay = exchange(pay, rest)
     pay = call(
-        relay_kernel, out_shape=jax.ShapeDtypeStruct((group_size(rest), PAY, 1, 128), F32), name="relay"
+        relay_kernel, out_shape=jax.ShapeDtypeStruct((group_size(line), PAY, 1, 128), F32), name="relay"
     )(pay)
-    pay = exchange(pay, rest)
+    pay = exchange(pay, line)
     return call(
         functools.partial(output_kernel, count=count),
         out_shape=jax.ShapeDtypeStruct((cx, cy, merged), BF16),

time: 72.7 us -> 68.7 us (0.945)
  the two profiles are of different devices: /device:TPU:1 before, /device:TPU:32 now
where the time goes in v5:
time: 68.7 us; the launch traced here: 68.4 us
  blocking collectives  43.2 us (63%)
  starting transfers between devices  12.5 us (18%)
  Pallas kernels  7.73 us (11%)
  waiting for transfers between devices  3.04 us (4%)
  local copies, waits for them, and re-layouts  1.86 us (3%)
    all_to_all x2, blocking collectives, exchange(): return lax.all_to_all(block, axes, 0, 0, tiled=True)  43.2 us
    ppermute x4, starting transfers between devices, swap(): lax.ppermute(block, axis, pairs + [(target, source) for source, target in...  12.5 us
    pallas_call x1, Pallas kernels, local(): call(functools.partial(output_kernel, count=count), out_shape=jax.ShapeDt...  4.33 us
    ppermute x4, waiting for transfers between devices, swap(): lax.ppermute(block, axis, pairs + [(target, source) for source, target in...  3.04 us
    pallas_call x1, Pallas kernels, local(): call(hidden_kernel, out_shape=(jax.ShapeDtypeStruct((cx + 2, cy + 2, rows...  2.41 us
    unnamed x12, local copies, waits for them, and re-layouts  1.86 us
  transfers between devices with their start and end apart: 4, of which 2 were waited for; matrix products, arithmetic and copies ran while one was open for 0% of the time, Pallas kernels for 1%

profile of v5, /device:TPU:32, one launch (start us, length us, event | category | flops | bytes accessed | tf_op | source)
XLA Modules:
  0.0 68.4 jit_solution(7365920793014971993)
XLA Ops:
  0.0 0.0 copy-start.1
  0.0 4.6 %collective-permute-start.1 = (bf16[2,8,4096]{2,1,0:T(8,128)(2,1)}, bf16[2,8,4096]{2,1,0:T(8,128)(2,1)S(1)}, u32[]{:S(2)}, u32[]{:S(2)}) collective-permute-start(bf16[2,8,4096]{2,1,0:T(8,128)(2,1)} %v_ref.1), channel_id=1, source_target_pairs={{8,16},{24,32},{40,48},{56,64},{72,80},{88,96},{104,112},{120,128}... | collective-permute-start | bytes 393224 | tf_op jit(solution)/shard_map/ppermute | solution.py:31
  4.6 2.5 %collective-permute-start = (bf16[2,8,4096]{2,1,0:T(8,128)(2,1)}, bf16[2,8,4096]{2,1,0:T(8,128)(2,1)S(1)}, u32[]{:S(2)}, u32[]{:S(2)}) collective-permute-start(bf16[2,8,4096]{2,1,0:T(8,128)(2,1)} %v_ref.1), channel_id=1, source_target_pairs={{0,8},{16,24},{32,40},{48,56},{64,72},{80,88},{96,104},{112,120},{... | collective-permute-start | bytes 393224 | tf_op jit(solution)/shard_map/ppermute | solution.py:31
  7.1 0.0 copy-start.2
  7.1 0.9 %copy-done.2 = bf16[2,8,4096]{2,1,0:T(8,128)(2,1)S(1)} copy-done((bf16[2,8,4096]{2,1,0:T(8,128)(2,1)S(1)}, bf16[2,8,4096]{2,1,0:T(8,128)(2,1)}, u32[]{:S(2)}) %copy-start.2) | copy-done | bytes 131096
  8.0 0.1 rows.1.own_ref
  8.1 0.0 copy-start
  8.1 0.9 %copy-done = bf16[1728,64]{0,1:T(8,128)(2,1)S(1)} copy-done((bf16[1728,64]{0,1:T(8,128)(2,1)S(1)}, bf16[1728,64]{0,1:T(8,128)(2,1)}, u32[]{:S(2)}) %copy-start) | copy-done | bytes 221208
  9.1 0.2 band.2.w_ref
  9.3 0.0 copy-done.1
  9.3 0.2 band.3.w_ref
  9.5 0.0 collective-permute-done.1.xb_ref
  9.6 2.1 %collective-permute-done.xa_ref = bf16[2,8,4096]{2,1,0:T(8,128)(2,1)S(1)} collective-permute-done((bf16[2,8,4096]{2,1,0:T(8,128)(2,1)}, bf16[2,8,4096]{2,1,0:T(8,128)(2,1)S(1)}, u32[]{:S(2)}, u32[]{:S(2)}) %collective-permute-start) | collective-permute-done | bytes 131104 | tf_op jit(solution)/shard_map/ppermute | solution.py:31
  11.7 0.2 edges.1
  11.9 0.7 collective-permute-start.2
  12.6 4.8 %collective-permute-start.3 = (bf16[6,2,16,256]{3,2,1,0:T(8,128)(2,1)S(1)}, bf16[6,2,16,256]{3,2,1,0:T(8,128)(2,1)S(1)}, u32[]{:S(2)}, u32[]{:S(2)}) collective-permute-start(bf16[6,2,16,256]{3,2,1,0:T(8,128)(2,1)S(1)} %get-tuple-element.16), channel_id=1, source_target_pairs={{0,1},{2,3},{4,5},{6,7},{1,0},{3,2},{5,4},{7,6},{8,9},{10,11},{12,... | collective-permute-start | bytes 294920 | tf_op jit(solution)/shard_map/ppermute | solution.py:31
  17.3 0.0 collective-permute-done.2.yb_ref
  17.3 0.9 %collective-permute-done.3.ya_ref = bf16[6,2,16,256]{3,2,1,0:T(8,128)(2,1)S(1)} collective-permute-done((bf16[6,2,16,256]{3,2,1,0:T(8,128)(2,1)S(1)}, bf16[6,2,16,256]{3,2,1,0:T(8,128)(2,1)S(1)}, u32[]{:S(2)}, u32[]{:S(2)}) %collective-permute-start.3) | collective-permute-done | bytes 98336 | tf_op jit(solution)/shard_map/ppermute | solution.py:31
  18.3 0.0 copy-start.3
  18.3 0.0 copy-start.4
  18.3 0.0 copy-start.5
  18.3 2.4 %hidden.1 = (f32[4,10,16,256]{3,2,1,0:T(8,128)S(1)}, f32[32,17,1,128]{3,2,1,0:T(1,128)S(1)}) custom-call(bf16[2,8,16,256]{3,2,1,0:T(8,128)(2,1)S(1)} %rows.1.own_ref, bf16[2,2,8,16,256]{4,3,2,1,0:T(8,128)(2,1)S(1)} %get-tuple-element.14.xs_ref, bf16[6,2,16,256]{3,2,1,0:T(8,128)(2,1)S(1)} %collective-permute-done.2.yb_ref, ...), custom_call_target="tpu_custom_call" | custom-call | tf_op jit(solution)/shard_map/hidden/pallas_call | solution.py:289
  20.7 14.7 %all_to_all.10.in_ref = f32[32,17,1,128]{3,2,1,0:T(1,128)S(1)} all-to-all(f32[32,17,1,128]{3,2,1,0:T(1,128)S(1)} %get-tuple-element.18), channel_id=1, replica_groups=mesh['gx_0'=16,'gx_1'=4,'gy_0'=4,'gy_1'=2] {'gx_1','gy_0','gy_1'}, dimensions={0} | all-to-all | bytes 557056 | tf_op jit(solution)/shard_map/all_to_all | solution.py:263
  35.4 0.2 relay.1
  35.6 28.4 %all_to_all.11.pay_ref = f32[16,17,1,128]{3,2,1,0:T(1,128)S(1)} all-to-all(f32[16,17,1,128]{3,2,1,0:T(1,128)S(1)} %relay.1), channel_id=1, replica_groups=mesh['gx_0'=16,'gx_1'=4,'gy_0'=4,'gy_1'=2] {'gx_0'}, dimensions={0} | all-to-all | bytes 278528 | tf_op jit(solution)/shard_map/all_to_all | solution.py:263
  64.1 0.0 copy-done.3
  64.1 0.0 copy-done.4
  64.1 0.0 copy-done.5
  64.1 4.3 %output.1 = bf16[2,8,4096]{2,1,0:T(8,128)(2,1)} custom-call(f32[16,17,1,128]{3,2,1,0:T(1,128)S(1)} %all_to_all.11.pay_ref, f32[4,10,16,256]{3,2,1,0:T(8,128)S(1)} %get-tuple-element.19.hidden_ref, f32[1,64]{1,0:T(1,128)S(1)} %bitcast.7, f32[1,64]{1,0:T(1,128)S(1)} %bitcast.8, bf16[256,3456]{1,0:T(8,128)(2,1)S(1)} %band.3.w_ref, f32[1,64]{1,0:T(1,128)S(1)} %bitcast.9), custom_call_target="tpu_custom_call" | custom-call | tf_op jit(solution)/shard_map/output/pallas_call | solution.py:307
Async XLA Ops:
  0.0 9.3 %copy-start.1 = (bf16[1728,64]{0,1:T(8,128)(2,1)S(1)}, bf16[1728,64]{0,1:T(8,128)(2,1)}, u32[]{:S(2)}) copy-start(bf16[1728,64]{0,1:T(8,128)(2,1)} %param.10) | copy-start | bytes 663556
  0.0 9.6 %collective-permute-start.1 = (bf16[2,8,4096]{2,1,0:T(8,128)(2,1)}, bf16[2,8,4096]{2,1,0:T(8,128)(2,1)S(1)}, u32[]{:S(2)}, u32[]{:S(2)}) collective-permute-start(bf16[2,8,4096]{2,1,0:T(8,128)(2,1)} %v_ref.1), channel_id=1, source_target_pairs={{8,16},{24,32},{40,48},{56,64},{72,80},{88,96},{104,112},{120,128}... | collective-permute-start | bytes 393224 | tf_op jit(solution)/shard_map/ppermute | solution.py:31
  4.6 7.1 %collective-permute-start = (bf16[2,8,4096]{2,1,0:T(8,128)(2,1)}, bf16[2,8,4096]{2,1,0:T(8,128)(2,1)S(1)}, u32[]{:S(2)}, u32[]{:S(2)}) collective-permute-start(bf16[2,8,4096]{2,1,0:T(8,128)(2,1)} %v_ref.1), channel_id=1, source_target_pairs={{0,8},{16,24},{32,40},{48,56},{64,72},{80,88},{96,104},{112,120},{... | collective-permute-start | bytes 393224 | tf_op jit(solution)/shard_map/ppermute | solution.py:31
  7.1 0.9 %copy-start.2 = (bf16[2,8,4096]{2,1,0:T(8,128)(2,1)S(1)}, bf16[2,8,4096]{2,1,0:T(8,128)(2,1)}, u32[]{:S(2)}) copy-start(bf16[2,8,4096]{2,1,0:T(8,128)(2,1)} %v_ref.1) | copy-start | bytes 393220
  8.1 0.9 %copy-start = (bf16[1728,64]{0,1:T(8,128)(2,1)S(1)}, bf16[1728,64]{0,1:T(8,128)(2,1)}, u32[]{:S(2)}) copy-start(bf16[1728,64]{0,1:T(8,128)(2,1)} %param.7) | copy-start | bytes 663556
  11.9 5.4 %collective-permute-start.2 = (bf16[6,2,16,256]{3,2,1,0:T(8,128)(2,1)S(1)}, bf16[6,2,16,256]{3,2,1,0:T(8,128)(2,1)S(1)}, u32[]{:S(2)}, u32[]{:S(2)}) collective-permute-start(bf16[6,2,16,256]{3,2,1,0:T(8,128)(2,1)S(1)} %get-tuple-element.15), channel_id=1, source_target_pairs={{1,2},{3,4},{5,6},{2,1},{4,3},{6,5},{9,10},{11,12},{13,14},{10,9},... | collective-permute-start | bytes 294920 | tf_op jit(solution)/shard_map/ppermute | solution.py:31
  12.6 5.7 %collective-permute-start.3 = (bf16[6,2,16,256]{3,2,1,0:T(8,128)(2,1)S(1)}, bf16[6,2,16,256]{3,2,1,0:T(8,128)(2,1)S(1)}, u32[]{:S(2)}, u32[]{:S(2)}) collective-permute-start(bf16[6,2,16,256]{3,2,1,0:T(8,128)(2,1)S(1)} %get-tuple-element.16), channel_id=1, source_target_pairs={{0,1},{2,3},{4,5},{6,7},{1,0},{3,2},{5,4},{7,6},{8,9},{10,11},{12,... | collective-permute-start | bytes 294920 | tf_op jit(solution)/shard_map/ppermute | solution.py:31
  18.3 45.8 %copy-start.3 = (f32[64]{0:T(128)S(1)}, f32[64]{0:T(128)}, u32[]{:S(2)}) copy-start(f32[64]{0:T(128)} %param.8) | copy-start | bytes 772
  18.3 45.8 %copy-start.4 = (f32[64]{0:T(128)S(1)}, f32[64]{0:T(128)}, u32[]{:S(2)}) copy-start(f32[64]{0:T(128)} %param.9) | copy-start | bytes 772
  18.3 45.8 %copy-start.5 = (f32[64]{0:T(128)S(1)}, f32[64]{0:T(128)}, u32[]{:S(2)}) copy-start(f32[64]{0:T(128)} %param.11) | copy-start | bytes 772

commit v6 on v5

--- a/solution.py
+++ b/solution.py
@@ -15,7 +15,7 @@
 F32 = jnp.float32
 BF16 = jnp.bfloat16
 HIGHEST = lax.Precision.HIGHEST
-PAY = 17
+PAY = 24
 
 
 def params():
@@ -132,7 +132,7 @@
     return total
 
 
-def hidden_kernel(own_ref, xs_ref, yb_ref, ya_ref, w_ref, hidden_ref, pay_ref, f_ref, x_ref):
+def hidden_kernel(own_ref, xs_ref, yb_ref, ya_ref, w_ref, hidden_ref, pay_ref, f_ref, x_ref, p_ref):
     rows = own_ref.shape[2]
     cx, cy = own_ref.shape[:2]
     clear_ends(f_ref, rows)
@@ -155,53 +155,53 @@
         lax.dot_general, dimension_numbers=(((0,), (0,)), ((), ())), preferred_element_type=F32
     )
     mixed = fold_blocks(outer(high, low))
-    i, j = square_iota(64)
-    column = jnp.sum(jnp.where(i == j, total, 0.0), axis=1, keepdims=True)
-    gram = fold_blocks(outer(high, high)) + (mixed + transposed(mixed)) + column * (total / cells)
+    gram = fold_blocks(outer(high, high)) + (mixed + transposed(mixed))
+    pack(gram, total, pay_ref, p_ref)
+
+
+def pack(cov, total, pay_ref, p_ref):
     i, j = square_iota(32)
-    low = gram[32:, 32:]
-    tri = jnp.where(j >= i, gram[:32, :32], low)
-    cross = gram[:32, 32:]
-    block = jnp.concatenate([tri[:16], tri[16:], cross[:16], cross[16:]], axis=1)
-    diag = jnp.sum(jnp.where(i == j, low, 0.0), axis=0, keepdims=True)
-    last = jnp.concatenate([diag, total, jnp.zeros((1, 32), F32)], axis=1)
+    low = cov[32:, 32:]
+    tri = jnp.where(j >= i, cov[:32, :32], low)
+    cross = cov[:32, 32:]
+    p_ref[0:16, :] = jnp.concatenate([tri[:16], tri[16:], cross[:16], cross[16:]], axis=1)
+    p_ref[16:24, :] = jnp.zeros((8, 128), F32)
+    p_ref[16:17, 0:32] = jnp.sum(jnp.where(i == j, low, 0.0), axis=0, keepdims=True)
+    for r in range(16, 19):
+        part = total.astype(BF16).astype(F32)
+        p_ref[r : r + 1, 32:96] = part
+        total = total - part
+    block = p_ref[...].astype(BF16)
     for p in range(pay_ref.shape[0]):
-        for r in range(16):
-            pay_ref[p, r] = block[r : r + 1]
-        pay_ref[p, 16] = last
-
-
-def relay_kernel(in_ref, out_ref):
-    total = jnp.sum(in_ref[...], axis=0)
-    for p in range(out_ref.shape[0]):
-        out_ref[p] = total
-
-
-def moments(pay_ref, p_ref, count):
-    total = jnp.sum(pay_ref[...], axis=0)
-    for r in range(PAY):
-        p_ref[r : r + 1, :] = total[r]
+        pay_ref[p] = block
+
+
+def combine(pay_ref, p_ref, cells):
+    each = pay_ref[...].astype(F32)
+    p_ref[...] = jnp.sum(each, axis=0)
     block = p_ref[0:16, :]
-    last = p_ref[16:17, :]
+    diag = p_ref[16:17, 0:32]
+    sums = jnp.sum(each[:, 16:24, :], axis=1)[:, 32:96]
+    total = jnp.sum(sums, axis=0, keepdims=True)
+    apart = sums / cells - total / (cells * pay_ref.shape[0])
+    between = lax.dot_general(
+        apart, apart * cells, (((0,), (0,)), ((), ())), precision=HIGHEST, preferred_element_type=F32
+    )
     i, j = square_iota(32)
     tri = jnp.concatenate([block[:, 0:32], block[:, 32:64]], axis=0)
     cross = jnp.concatenate([block[:, 64:96], block[:, 96:128]], axis=0)
     flip = transposed(tri)
     top = jnp.where(j >= i, tri, flip)
     low = jnp.where(j < i, tri, flip)
-    low = jnp.where(i == j, jnp.broadcast_to(last[:, 0:32], (32, 32)), low)
-    gram = jnp.concatenate(
-        [
-            jnp.concatenate([top, cross], axis=1),
-            jnp.concatenate([transposed(cross), low], axis=1),
-        ],
-        axis=0,
-    )
-    mean = last[:, 32:96] / count
-    i, j = square_iota(64)
-    eye = jnp.where(i == j, 1.0, 0.0).astype(F32)
-    column = jnp.sum(eye * mean, axis=1, keepdims=True)
-    return mean, gram / count - column * mean + 1e-05 * eye, eye
+    low = jnp.where(i == j, jnp.broadcast_to(diag, (32, 32)), low)
+    upper = jnp.concatenate([top, cross], axis=1)
+    lower = jnp.concatenate([transposed(cross), low], axis=1)
+    return jnp.concatenate([upper, lower], axis=0) + between, total
+
+
+def relay_kernel(in_ref, out_ref, p_ref, *, cells):
+    cov, total = combine(in_ref, p_ref, cells)
+    pack(cov, total, out_ref, p_ref)
 
 
 def newton_whiten(sigma, eye):
@@ -218,7 +218,11 @@
     pay_ref, hidden_ref, gain_ref, shift_ref, w_ref, bias_ref, out_ref, p_ref, f_ref, x_ref, o_ref, *, count
 ):
     nx, ny, rows, lanes = hidden_ref.shape
-    mean, sigma, eye = moments(pay_ref, p_ref, count)
+    cov, total = combine(pay_ref, p_ref, count / pay_ref.shape[0])
+    i, j = square_iota(64)
+    eye = jnp.where(i == j, 1.0, 0.0).astype(F32)
+    mean = total / count
+    sigma = cov / count + 1e-05 * eye
     whiten = newton_whiten(sigma, eye)
     i, j = square_iota(lanes)
     wide = jnp.concatenate([whiten] * PACK, axis=1)
@@ -269,6 +273,8 @@
     lanes = PACK * width
     rows = merged // lanes
     count = float(cx * group_size(GX) * cy * group_size(GY) * (merged // width))
+    rest, line = GX[1:] + GY, GX[:1]
+    packed = pltpu.VMEM((PAY, 128), F32)
     call = functools.partial(pl.pallas_call, compiler_params=params())
     xa, xb = swap(volume, GX, 0), swap(volume, GX, 1)
     block = jax.ShapeDtypeStruct((cx, cy, rows, lanes), BF16)
@@ -290,25 +296,28 @@
         hidden_kernel,
         out_shape=(
             jax.ShapeDtypeStruct((cx + 2, cy + 2, rows, lanes), F32),
-            jax.ShapeDtypeStruct((group_size(GX[1:] + GY), PAY, 1, 128), F32),
+            jax.ShapeDtypeStruct((group_size(rest), PAY, 128), BF16),
         ),
         scratch_shapes=[
             pltpu.VMEM((cx + 4, cy + 4, rows + 16, lanes), F32),
             pltpu.VMEM((cx + 4, cy + 4, rows, 6 * width), BF16),
+            packed,
         ],
         name="hidden",
     )(own, xs, yb, ya, first)
-    rest, line = GX[1:] + GY, GX[:1]
     pay = exchange(pay, rest)
     pay = call(
-        relay_kernel, out_shape=jax.ShapeDtypeStruct((group_size(line), PAY, 1, 128), F32), name="relay"
+        functools.partial(relay_kernel, cells=float(cx * cy * (merged // width))),
+        out_shape=jax.ShapeDtypeStruct((group_size(line), PAY, 128), BF16),
+        scratch_shapes=[packed],
+        name="relay",
     )(pay)
     pay = exchange(pay, line)
     return call(
         functools.partial(output_kernel, count=count),
         out_shape=jax.ShapeDtypeStruct((cx, cy, merged), BF16),
         scratch_shapes=[
-            pltpu.VMEM((24, 128), F32),
+            packed,
             pltpu.VMEM((cx + 2, cy + 2, rows + 16, lanes), F32),
             pltpu.VMEM((cx + 2, cy + 2, rows, 6 * width), BF16),
             pltpu.VMEM((lanes // 128, cx * cy * rows, 128), F32),

time: 68.7 us -> 67.2 us (0.978)
  the two profiles are of different devices: /device:TPU:32 before, /device:TPU:1 now
where the time goes in v6:
time: 67.2 us; the launch traced here: 66.5 us
  blocking collectives  40.8 us (61%)
  starting transfers between devices  14.8 us (22%)
  Pallas kernels  8 us (12%)
  local copies, waits for them, and re-layouts  1.86 us (3%)
  waiting for transfers between devices  0.98 us (1%)
    all_to_all x2, blocking collectives, exchange(): return lax.all_to_all(block, axes, 0, 0, tiled=True)  40.8 us
    ppermute x4, starting transfers between devices, swap(): lax.ppermute(block, axis, pairs + [(target, source) for source, target in...  14.8 us
    pallas_call x1, Pallas kernels, local(): call(functools.partial(output_kernel, count=count), out_shape=jax.ShapeDt...  4.33 us
    pallas_call x1, Pallas kernels, local(): call(hidden_kernel, out_shape=(jax.ShapeDtypeStruct((cx + 2, cy + 2, rows...  2.4 us
    unnamed x12, local copies, waits for them, and re-layouts  1.86 us
  transfers between devices with their start and end apart: 4, of which 2 were waited for; matrix products, arithmetic and copies ran while one was open for 0% of the time, Pallas kernels for 1%

profile of v6, /device:TPU:1, one launch (start us, length us, event | category | flops | bytes accessed | tf_op | source)
XLA Modules:
  0.0 66.5 jit_solution(13003782983291825568)
XLA Ops:
  0.0 0.0 copy-start.1
  0.0 0.8 %collective-permute-start.1 = (bf16[2,8,4096]{2,1,0:T(8,128)(2,1)}, bf16[2,8,4096]{2,1,0:T(8,128)(2,1)S(1)}, u32[]{:S(2)}, u32[]{:S(2)}) collective-permute-start(bf16[2,8,4096]{2,1,0:T(8,128)(2,1)} %v_ref.1), channel_id=1, source_target_pairs={{8,16},{24,32},{40,48},{56,64},{72,80},{88,96},{104,112},{120,128}... | collective-permute-start | bytes 393224 | tf_op jit(solution)/shard_map/ppermute | solution.py:31
  0.8 6.6 %collective-permute-start = (bf16[2,8,4096]{2,1,0:T(8,128)(2,1)}, bf16[2,8,4096]{2,1,0:T(8,128)(2,1)S(1)}, u32[]{:S(2)}, u32[]{:S(2)}) collective-permute-start(bf16[2,8,4096]{2,1,0:T(8,128)(2,1)} %v_ref.1), channel_id=1, source_target_pairs={{0,8},{16,24},{32,40},{48,56},{64,72},{80,88},{96,104},{112,120},{... | collective-permute-start | bytes 393224 | tf_op jit(solution)/shard_map/ppermute | solution.py:31
  7.4 0.0 copy-start.2
  7.4 0.9 %copy-done.2 = bf16[2,8,4096]{2,1,0:T(8,128)(2,1)S(1)} copy-done((bf16[2,8,4096]{2,1,0:T(8,128)(2,1)S(1)}, bf16[2,8,4096]{2,1,0:T(8,128)(2,1)}, u32[]{:S(2)}) %copy-start.2) | copy-done | bytes 131096
  8.3 0.1 rows.1.own_ref
  8.4 0.0 copy-start
  8.4 0.9 %copy-done = bf16[1728,64]{0,1:T(8,128)(2,1)S(1)} copy-done((bf16[1728,64]{0,1:T(8,128)(2,1)S(1)}, bf16[1728,64]{0,1:T(8,128)(2,1)}, u32[]{:S(2)}) %copy-start) | copy-done | bytes 221208
  9.3 0.2 band.2.w_ref
  9.6 0.0 copy-done.1
  9.6 0.2 band.3.w_ref
  9.8 0.0 copy-start.3
  9.8 0.0 copy-start.4
  9.8 0.0 copy-start.5
  9.9 0.0 collective-permute-done.1.xb_ref
  9.9 0.1 collective-permute-done.xa_ref
  9.9 0.2 edges.1
  10.2 5.1 %collective-permute-start.2 = (bf16[6,2,16,256]{3,2,1,0:T(8,128)(2,1)S(1)}, bf16[6,2,16,256]{3,2,1,0:T(8,128)(2,1)S(1)}, u32[]{:S(2)}, u32[]{:S(2)}) collective-permute-start(bf16[6,2,16,256]{3,2,1,0:T(8,128)(2,1)S(1)} %get-tuple-element.15), channel_id=1, source_target_pairs={{1,2},{3,4},{5,6},{2,1},{4,3},{6,5},{9,10},{11,12},{13,14},{10,9},... | collective-permute-start | bytes 294920 | tf_op jit(solution)/shard_map/ppermute | solution.py:31
  15.3 2.3 %collective-permute-start.3 = (bf16[6,2,16,256]{3,2,1,0:T(8,128)(2,1)S(1)}, bf16[6,2,16,256]{3,2,1,0:T(8,128)(2,1)S(1)}, u32[]{:S(2)}, u32[]{:S(2)}) collective-permute-start(bf16[6,2,16,256]{3,2,1,0:T(8,128)(2,1)S(1)} %get-tuple-element.16), channel_id=1, source_target_pairs={{0,1},{2,3},{4,5},{6,7},{1,0},{3,2},{5,4},{7,6},{8,9},{10,11},{12,... | collective-permute-start | bytes 294920 | tf_op jit(solution)/shard_map/ppermute | solution.py:31
  17.6 0.0 collective-permute-done.2.yb_ref
  17.6 0.9 %collective-permute-done.3.ya_ref = bf16[6,2,16,256]{3,2,1,0:T(8,128)(2,1)S(1)} collective-permute-done((bf16[6,2,16,256]{3,2,1,0:T(8,128)(2,1)S(1)}, bf16[6,2,16,256]{3,2,1,0:T(8,128)(2,1)S(1)}, u32[]{:S(2)}, u32[]{:S(2)}) %collective-permute-start.3) | collective-permute-done | bytes 98336 | tf_op jit(solution)/shard_map/ppermute | solution.py:31
  18.5 2.4 %hidden.1 = (f32[4,10,16,256]{3,2,1,0:T(8,128)S(1)}, bf16[32,24,128]{2,1,0:T(8,128)(2,1)S(1)}) custom-call(bf16[2,8,16,256]{3,2,1,0:T(8,128)(2,1)S(1)} %rows.1.own_ref, bf16[2,2,8,16,256]{4,3,2,1,0:T(8,128)(2,1)S(1)} %get-tuple-element.14.xs_ref, bf16[6,2,16,256]{3,2,1,0:T(8,128)(2,1)S(1)} %collective-permute-done.2.yb_ref, ...), custom_call_target="tpu_custom_call" | custom-call | tf_op jit(solution)/shard_map/hidden/pallas_call | solution.py:295
  20.9 15.0 %all_to_all.10.in_ref = bf16[32,24,128]{2,1,0:T(8,128)(2,1)S(1)} all-to-all(bf16[32,24,128]{2,1,0:T(8,128)(2,1)S(1)} %get-tuple-element.18), channel_id=1, replica_groups=mesh['gx_0'=16,'gx_1'=4,'gy_0'=4,'gy_1'=2] {'gx_1','gy_0','gy_1'}, dimensions={0} | all-to-all | bytes 393216 | tf_op jit(solution)/shard_map/all_to_all | solution.py:267
  35.9 0.5 relay.1
  36.4 25.8 %all_to_all.11.pay_ref = bf16[16,24,128]{2,1,0:T(8,128)(2,1)S(1)} all-to-all(bf16[16,24,128]{2,1,0:T(8,128)(2,1)S(1)} %relay.1), channel_id=1, replica_groups=mesh['gx_0'=16,'gx_1'=4,'gy_0'=4,'gy_1'=2] {'gx_0'}, dimensions={0} | all-to-all | bytes 196608 | tf_op jit(solution)/shard_map/all_to_all | solution.py:267
  62.2 0.0 copy-done.3
  62.2 0.0 copy-done.4
  62.2 0.0 copy-done.5
  62.2 4.3 %output.1 = bf16[2,8,4096]{2,1,0:T(8,128)(2,1)} custom-call(bf16[16,24,128]{2,1,0:T(8,128)(2,1)S(1)} %all_to_all.11.pay_ref, f32[4,10,16,256]{3,2,1,0:T(8,128)S(1)} %get-tuple-element.19.hidden_ref, f32[1,64]{1,0:T(1,128)S(1)} %bitcast.7, f32[1,64]{1,0:T(1,128)S(1)} %bitcast.8, bf16[256,3456]{1,0:T(8,128)(2,1)S(1)} %band.3.w_ref, f32[1,64]{1,0:T(1,128)S(1)} %bitcast.9), custom_call_target="tpu_custom_call" | custom-call | tf_op jit(solution)/shard_map/output/pallas_call | solution.py:316
Async XLA Ops:
  0.0 9.6 %copy-start.1 = (bf16[1728,64]{0,1:T(8,128)(2,1)S(1)}, bf16[1728,64]{0,1:T(8,128)(2,1)}, u32[]{:S(2)}) copy-start(bf16[1728,64]{0,1:T(8,128)(2,1)} %param.10) | copy-start | bytes 663556
  0.0 9.9 %collective-permute-start.1 = (bf16[2,8,4096]{2,1,0:T(8,128)(2,1)}, bf16[2,8,4096]{2,1,0:T(8,128)(2,1)S(1)}, u32[]{:S(2)}, u32[]{:S(2)}) collective-permute-start(bf16[2,8,4096]{2,1,0:T(8,128)(2,1)} %v_ref.1), channel_id=1, source_target_pairs={{8,16},{24,32},{40,48},{56,64},{72,80},{88,96},{104,112},{120,128}... | collective-permute-start | bytes 393224 | tf_op jit(solution)/shard_map/ppermute | solution.py:31
  0.8 9.1 %collective-permute-start = (bf16[2,8,4096]{2,1,0:T(8,128)(2,1)}, bf16[2,8,4096]{2,1,0:T(8,128)(2,1)S(1)}, u32[]{:S(2)}, u32[]{:S(2)}) collective-permute-start(bf16[2,8,4096]{2,1,0:T(8,128)(2,1)} %v_ref.1), channel_id=1, source_target_pairs={{0,8},{16,24},{32,40},{48,56},{64,72},{80,88},{96,104},{112,120},{... | collective-permute-start | bytes 393224 | tf_op jit(solution)/shard_map/ppermute | solution.py:31
  7.4 0.9 %copy-start.2 = (bf16[2,8,4096]{2,1,0:T(8,128)(2,1)S(1)}, bf16[2,8,4096]{2,1,0:T(8,128)(2,1)}, u32[]{:S(2)}) copy-start(bf16[2,8,4096]{2,1,0:T(8,128)(2,1)} %v_ref.1) | copy-start | bytes 393220
  8.4 0.9 %copy-start = (bf16[1728,64]{0,1:T(8,128)(2,1)S(1)}, bf16[1728,64]{0,1:T(8,128)(2,1)}, u32[]{:S(2)}) copy-start(bf16[1728,64]{0,1:T(8,128)(2,1)} %param.7) | copy-start | bytes 663556
  9.8 52.3 %copy-start.3 = (f32[64]{0:T(128)S(1)}, f32[64]{0:T(128)}, u32[]{:S(2)}) copy-start(f32[64]{0:T(128)} %param.8) | copy-start | bytes 772
  9.8 52.3 %copy-start.4 = (f32[64]{0:T(128)S(1)}, f32[64]{0:T(128)}, u32[]{:S(2)}) copy-start(f32[64]{0:T(128)} %param.9) | copy-start | bytes 772
  9.8 52.3 %copy-start.5 = (f32[64]{0:T(128)S(1)}, f32[64]{0:T(128)}, u32[]{:S(2)}) copy-start(f32[64]{0:T(128)} %param.11) | copy-start | bytes 772
  10.2 7.4 %collective-permute-start.2 = (bf16[6,2,16,256]{3,2,1,0:T(8,128)(2,1)S(1)}, bf16[6,2,16,256]{3,2,1,0:T(8,128)(2,1)S(1)}, u32[]{:S(2)}, u32[]{:S(2)}) collective-permute-start(bf16[6,2,16,256]{3,2,1,0:T(8,128)(2,1)S(1)} %get-tuple-element.15), channel_id=1, source_target_pairs={{1,2},{3,4},{5,6},{2,1},{4,3},{6,5},{9,10},{11,12},{13,14},{10,9},... | collective-permute-start | bytes 294920 | tf_op jit(solution)/shard_map/ppermute | solution.py:31
  15.3 3.2 %collective-permute-start.3 = (bf16[6,2,16,256]{3,2,1,0:T(8,128)(2,1)S(1)}, bf16[6,2,16,256]{3,2,1,0:T(8,128)(2,1)S(1)}, u32[]{:S(2)}, u32[]{:S(2)}) collective-permute-start(bf16[6,2,16,256]{3,2,1,0:T(8,128)(2,1)S(1)} %get-tuple-element.16), channel_id=1, source_target_pairs={{0,1},{2,3},{4,5},{6,7},{1,0},{3,2},{5,4},{7,6},{8,9},{10,11},{12,... | collective-permute-start | bytes 294920 | tf_op jit(solution)/shard_map/ppermute | solution.py:31

commit v7 on v5

--- a/solution.py
+++ b/solution.py
@@ -84,20 +84,22 @@
 
 def clear_ends(f_ref, rows):
     cells_x, cells_y, _, lanes = f_ref.shape
-    zero = jnp.zeros((cells_x, cells_y, 8, lanes), F32)
-    f_ref[:, :, 0:8, :] = zero
-    f_ref[:, :, 8 + rows : 16 + rows, :] = zero
+    zero = jnp.zeros((cells_x, cells_y, 1, lanes // 2), F32)
+    f_ref[:, :, 7:8, lanes // 2 :] = zero
+    f_ref[:, :, 8 + rows : 9 + rows, : lanes // 2] = zero
 
 
 def banded_conv(x_ref, w_ref):
     nx, ny, rows, k = x_ref.shape
     nx, ny = nx - 2, ny - 2
+    m = nx * ny * rows
+    taps = [x_ref[dx : dx + nx, dy : dy + ny].reshape(m, k) for dx in range(3) for dy in range(3)]
     acc = None
-    for dx in range(3):
-        taps = [x_ref[dx : dx + nx, dy : dy + ny].reshape(nx * ny * rows, k) for dy in range(3)]
+    for first in range(0, 9, 2):
+        last = min(first + 2, 9)
         part = lax.dot_general(
-            jnp.concatenate(taps, axis=1),
-            w_ref[:, dx * 3 * k : (dx + 1) * 3 * k],
+            jnp.concatenate(taps[first:last], axis=1),
+            w_ref[:, first * k : last * k],
             (((1,), (1,)), ((), ())),
             preferred_element_type=F32,
         )

time: 68.7 us -> 68.6 us (level)
  no operation moved by 1% of the time
where the time goes in v7:
time: 68.6 us; the launch traced here: 68.3 us
  blocking collectives  43.2 us (63%)
  starting transfers between devices  12.5 us (18%)
  Pallas kernels  7.61 us (11%)
  waiting for transfers between devices  3.04 us (4%)
  local copies, waits for them, and re-layouts  1.86 us (3%)
    all_to_all x2, blocking collectives, exchange(): return lax.all_to_all(block, axes, 0, 0, tiled=True)  43.2 us
    ppermute x4, starting transfers between devices, swap(): lax.ppermute(block, axis, pairs + [(target, source) for source, target in...  12.5 us
    pallas_call x1, Pallas kernels, local(): call(functools.partial(output_kernel, count=count), out_shape=jax.ShapeDt...  4.33 us
    ppermute x4, waiting for transfers between devices, swap(): lax.ppermute(block, axis, pairs + [(target, source) for source, target in...  3.04 us
    pallas_call x1, Pallas kernels, local(): call(hidden_kernel, out_shape=(jax.ShapeDtypeStruct((cx + 2, cy + 2, rows...  2.3 us
    unnamed x12, local copies, waits for them, and re-layouts  1.86 us
  transfers between devices with their start and end apart: 4, of which 2 were waited for; matrix products, arithmetic and copies ran while one was open for 0% of the time, Pallas kernels for 1%

profile of v7, /device:TPU:32, one launch (start us, length us, event | category | flops | bytes accessed | tf_op | source)
XLA Modules:
  0.0 68.3 jit_solution(18028246113495576904)
XLA Ops:
  0.0 0.0 copy-start.1
  0.0 4.6 %collective-permute-start.1 = (bf16[2,8,4096]{2,1,0:T(8,128)(2,1)}, bf16[2,8,4096]{2,1,0:T(8,128)(2,1)S(1)}, u32[]{:S(2)}, u32[]{:S(2)}) collective-permute-start(bf16[2,8,4096]{2,1,0:T(8,128)(2,1)} %v_ref.1), channel_id=1, source_target_pairs={{8,16},{24,32},{40,48},{56,64},{72,80},{88,96},{104,112},{120,128}... | collective-permute-start | bytes 393224 | tf_op jit(solution)/shard_map/ppermute | solution.py:31
  4.6 2.5 %collective-permute-start = (bf16[2,8,4096]{2,1,0:T(8,128)(2,1)}, bf16[2,8,4096]{2,1,0:T(8,128)(2,1)S(1)}, u32[]{:S(2)}, u32[]{:S(2)}) collective-permute-start(bf16[2,8,4096]{2,1,0:T(8,128)(2,1)} %v_ref.1), channel_id=1, source_target_pairs={{0,8},{16,24},{32,40},{48,56},{64,72},{80,88},{96,104},{112,120},{... | collective-permute-start | bytes 393224 | tf_op jit(solution)/shard_map/ppermute | solution.py:31
  7.1 0.0 copy-start.2
  7.1 0.9 %copy-done.2 = bf16[2,8,4096]{2,1,0:T(8,128)(2,1)S(1)} copy-done((bf16[2,8,4096]{2,1,0:T(8,128)(2,1)S(1)}, bf16[2,8,4096]{2,1,0:T(8,128)(2,1)}, u32[]{:S(2)}) %copy-start.2) | copy-done | bytes 131096
  8.0 0.1 rows.1.own_ref
  8.1 0.0 copy-start
  8.1 0.9 %copy-done = bf16[1728,64]{0,1:T(8,128)(2,1)S(1)} copy-done((bf16[1728,64]{0,1:T(8,128)(2,1)S(1)}, bf16[1728,64]{0,1:T(8,128)(2,1)}, u32[]{:S(2)}) %copy-start) | copy-done | bytes 221208
  9.1 0.2 band.2.w_ref
  9.3 0.0 copy-done.1
  9.3 0.2 band.3.w_ref
  9.5 0.0 collective-permute-done.1.xb_ref
  9.6 2.1 %collective-permute-done.xa_ref = bf16[2,8,4096]{2,1,0:T(8,128)(2,1)S(1)} collective-permute-done((bf16[2,8,4096]{2,1,0:T(8,128)(2,1)}, bf16[2,8,4096]{2,1,0:T(8,128)(2,1)S(1)}, u32[]{:S(2)}, u32[]{:S(2)}) %collective-permute-start) | collective-permute-done | bytes 131104 | tf_op jit(solution)/shard_map/ppermute | solution.py:31
  11.7 0.2 edges.1
  11.9 0.7 collective-permute-start.2
  12.6 4.8 %collective-permute-start.3 = (bf16[6,2,16,256]{3,2,1,0:T(8,128)(2,1)S(1)}, bf16[6,2,16,256]{3,2,1,0:T(8,128)(2,1)S(1)}, u32[]{:S(2)}, u32[]{:S(2)}) collective-permute-start(bf16[6,2,16,256]{3,2,1,0:T(8,128)(2,1)S(1)} %get-tuple-element.16), channel_id=1, source_target_pairs={{0,1},{2,3},{4,5},{6,7},{1,0},{3,2},{5,4},{7,6},{8,9},{10,11},{12,... | collective-permute-start | bytes 294920 | tf_op jit(solution)/shard_map/ppermute | solution.py:31
  17.3 0.0 collective-permute-done.2.yb_ref
  17.3 0.9 %collective-permute-done.3.ya_ref = bf16[6,2,16,256]{3,2,1,0:T(8,128)(2,1)S(1)} collective-permute-done((bf16[6,2,16,256]{3,2,1,0:T(8,128)(2,1)S(1)}, bf16[6,2,16,256]{3,2,1,0:T(8,128)(2,1)S(1)}, u32[]{:S(2)}, u32[]{:S(2)}) %collective-permute-start.3) | collective-permute-done | bytes 98336 | tf_op jit(solution)/shard_map/ppermute | solution.py:31
  18.3 0.0 copy-start.3
  18.3 0.0 copy-start.4
  18.3 0.0 copy-start.5
  18.3 2.3 %hidden.1 = (f32[4,10,16,256]{3,2,1,0:T(8,128)S(1)}, f32[32,17,1,128]{3,2,1,0:T(1,128)S(1)}) custom-call(bf16[2,8,16,256]{3,2,1,0:T(8,128)(2,1)S(1)} %rows.1.own_ref, bf16[2,2,8,16,256]{4,3,2,1,0:T(8,128)(2,1)S(1)} %get-tuple-element.14.xs_ref, bf16[6,2,16,256]{3,2,1,0:T(8,128)(2,1)S(1)} %collective-permute-done.2.yb_ref, ...), custom_call_target="tpu_custom_call" | custom-call | tf_op jit(solution)/shard_map/hidden/pallas_call | solution.py:291
  20.6 14.7 %all_to_all.10.in_ref = f32[32,17,1,128]{3,2,1,0:T(1,128)S(1)} all-to-all(f32[32,17,1,128]{3,2,1,0:T(1,128)S(1)} %get-tuple-element.18), channel_id=1, replica_groups=mesh['gx_0'=16,'gx_1'=4,'gy_0'=4,'gy_1'=2] {'gx_1','gy_0','gy_1'}, dimensions={0} | all-to-all | bytes 557056 | tf_op jit(solution)/shard_map/all_to_all | solution.py:265
  35.3 0.2 relay.1
  35.5 28.4 %all_to_all.11.pay_ref = f32[16,17,1,128]{3,2,1,0:T(1,128)S(1)} all-to-all(f32[16,17,1,128]{3,2,1,0:T(1,128)S(1)} %relay.1), channel_id=1, replica_groups=mesh['gx_0'=16,'gx_1'=4,'gy_0'=4,'gy_1'=2] {'gx_0'}, dimensions={0} | all-to-all | bytes 278528 | tf_op jit(solution)/shard_map/all_to_all | solution.py:265
  63.9 0.0 copy-done.3
  63.9 0.0 copy-done.4
  63.9 0.0 copy-done.5
  63.9 4.3 %output.1 = bf16[2,8,4096]{2,1,0:T(8,128)(2,1)} custom-call(f32[16,17,1,128]{3,2,1,0:T(1,128)S(1)} %all_to_all.11.pay_ref, f32[4,10,16,256]{3,2,1,0:T(8,128)S(1)} %get-tuple-element.19.hidden_ref, f32[1,64]{1,0:T(1,128)S(1)} %bitcast.7, f32[1,64]{1,0:T(1,128)S(1)} %bitcast.8, bf16[256,3456]{1,0:T(8,128)(2,1)S(1)} %band.3.w_ref, f32[1,64]{1,0:T(1,128)S(1)} %bitcast.9), custom_call_target="tpu_custom_call" | custom-call | tf_op jit(solution)/shard_map/output/pallas_call | solution.py:309
Async XLA Ops:
  0.0 9.3 %copy-start.1 = (bf16[1728,64]{0,1:T(8,128)(2,1)S(1)}, bf16[1728,64]{0,1:T(8,128)(2,1)}, u32[]{:S(2)}) copy-start(bf16[1728,64]{0,1:T(8,128)(2,1)} %param.10) | copy-start | bytes 663556
  0.0 9.6 %collective-permute-start.1 = (bf16[2,8,4096]{2,1,0:T(8,128)(2,1)}, bf16[2,8,4096]{2,1,0:T(8,128)(2,1)S(1)}, u32[]{:S(2)}, u32[]{:S(2)}) collective-permute-start(bf16[2,8,4096]{2,1,0:T(8,128)(2,1)} %v_ref.1), channel_id=1, source_target_pairs={{8,16},{24,32},{40,48},{56,64},{72,80},{88,96},{104,112},{120,128}... | collective-permute-start | bytes 393224 | tf_op jit(solution)/shard_map/ppermute | solution.py:31
  4.6 7.1 %collective-permute-start = (bf16[2,8,4096]{2,1,0:T(8,128)(2,1)}, bf16[2,8,4096]{2,1,0:T(8,128)(2,1)S(1)}, u32[]{:S(2)}, u32[]{:S(2)}) collective-permute-start(bf16[2,8,4096]{2,1,0:T(8,128)(2,1)} %v_ref.1), channel_id=1, source_target_pairs={{0,8},{16,24},{32,40},{48,56},{64,72},{80,88},{96,104},{112,120},{... | collective-permute-start | bytes 393224 | tf_op jit(solution)/shard_map/ppermute | solution.py:31
  7.1 0.9 %copy-start.2 = (bf16[2,8,4096]{2,1,0:T(8,128)(2,1)S(1)}, bf16[2,8,4096]{2,1,0:T(8,128)(2,1)}, u32[]{:S(2)}) copy-start(bf16[2,8,4096]{2,1,0:T(8,128)(2,1)} %v_ref.1) | copy-start | bytes 393220
  8.1 0.9 %copy-start = (bf16[1728,64]{0,1:T(8,128)(2,1)S(1)}, bf16[1728,64]{0,1:T(8,128)(2,1)}, u32[]{:S(2)}) copy-start(bf16[1728,64]{0,1:T(8,128)(2,1)} %param.7) | copy-start | bytes 663556
  11.9 5.4 %collective-permute-start.2 = (bf16[6,2,16,256]{3,2,1,0:T(8,128)(2,1)S(1)}, bf16[6,2,16,256]{3,2,1,0:T(8,128)(2,1)S(1)}, u32[]{:S(2)}, u32[]{:S(2)}) collective-permute-start(bf16[6,2,16,256]{3,2,1,0:T(8,128)(2,1)S(1)} %get-tuple-element.15), channel_id=1, source_target_pairs={{1,2},{3,4},{5,6},{2,1},{4,3},{6,5},{9,10},{11,12},{13,14},{10,9},... | collective-permute-start | bytes 294920 | tf_op jit(solution)/shard_map/ppermute | solution.py:31
  12.6 5.7 %collective-permute-start.3 = (bf16[6,2,16,256]{3,2,1,0:T(8,128)(2,1)S(1)}, bf16[6,2,16,256]{3,2,1,0:T(8,128)(2,1)S(1)}, u32[]{:S(2)}, u32[]{:S(2)}) collective-permute-start(bf16[6,2,16,256]{3,2,1,0:T(8,128)(2,1)S(1)} %get-tuple-element.16), channel_id=1, source_target_pairs={{0,1},{2,3},{4,5},{6,7},{1,0},{3,2},{5,4},{7,6},{8,9},{10,11},{12,... | collective-permute-start | bytes 294920 | tf_op jit(solution)/shard_map/ppermute | solution.py:31
  18.3 45.7 %copy-start.3 = (f32[64]{0:T(128)S(1)}, f32[64]{0:T(128)}, u32[]{:S(2)}) copy-start(f32[64]{0:T(128)} %param.8) | copy-start | bytes 772
  18.3 45.7 %copy-start.4 = (f32[64]{0:T(128)S(1)}, f32[64]{0:T(128)}, u32[]{:S(2)}) copy-start(f32[64]{0:T(128)} %param.9) | copy-start | bytes 772
  18.3 45.7 %copy-start.5 = (f32[64]{0:T(128)S(1)}, f32[64]{0:T(128)}, u32[]{:S(2)}) copy-start(f32[64]{0:T(128)} %param.11) | copy-start | bytes 772
